TPU v7x, 512 devices: a whole 4x4x16 slice. The times are simulated.
512 devices in a mesh: seq: 128 (over x_hi, y, z), dp: 4 (over x_lo, core).
Axes of the slice: x: 4 (x_hi: 2, x_lo: 2; x = x_hi * 2 + x_lo), y: 4, z: 16, core: 2. Of those that a mesh axis runs over, the one named last changes fastest.
Arguments:
- asking_vectors: bfloat16 [4, 16384, 2048], P('dp', 'seq'), may hold values from -100 to 100
- lookup_vectors: bfloat16 [4, 16384, 2048], P('dp', 'seq'), may hold values from -13 to 13
- payload_vectors: bfloat16 [4, 16384, 2048], P('dp', 'seq'), may hold values from -6 to 6
- incoming_sensitivity: bfloat16 [4, 16384, 2048], P('dp', 'seq'), may hold values from -6 to 6
- learned_sharpness: float32 [16], replicated, may hold values from 0.5 to 2
- reply_list_sizes: int32 [4, 8], P('dp'), may hold values from 1 to 8192, 16384 in all within a row
Outputs:
- attention_result: bfloat16 [4, 16384, 2048], P('dp', 'seq')
- query_gradient: bfloat16 [4, 16384, 2048], P('dp', 'seq')
- key_gradient: bfloat16 [4, 16384, 2048], P('dp', 'seq')
- value_gradient: bfloat16 [4, 16384, 2048], P('dp', 'seq')
- scale_gradient: float32 [16], replicated
All inputs are finite; a program needn't handle non-finite values.
Results may differ from a plain program's by a relative error of at most 0.02.
The roundings to bfloat16 on the way count: a program that leaves them out, or rounds other values in their place, can miss the bound.
Values may be sent and summed in bfloat16 or wider, within the bound.
No kernel may reach another device: no remote copies, remote signals or barrier semaphores. Data moves between devices by JAX's collectives and lax.ppermute only.
A program may use at most 64 MiB of HBM per device.

v0:
```python
import math
import jax
import jax.numpy as jnp
from jax import lax
from jax.sharding import PartitionSpec as P

MIXER_CHANNELS = 16


def partner(array, axis, apart):
    return lax.ppermute(array, axis, [(i, i ^ 1 << apart) for i in range(lax.axis_size(axis))])


def level_plan(level_idx, head_idx, seq_devices):
    group_span = min(2**level_idx, seq_devices)
    dilation = max(1, group_span // 4)
    offset = (5 + head_idx * (dilation // 2)) % dilation
    return (group_span, dilation, offset)


def body(
    asking_vectors,
    lookup_vectors,
    payload_vectors,
    incoming_sensitivity,
    learned_sharpness,
    reply_list_sizes,
):
    seq_devices = lax.axis_size("seq")
    device_idx = lax.axis_index("seq")
    tokens = asking_vectors.shape[1]
    channel_extent = asking_vectors.shape[2] // MIXER_CHANNELS
    level_count = MIXER_CHANNELS // 2
    queries = asking_vectors[0]
    keyed = lookup_vectors[0]
    valued = payload_vectors[0]
    upstream = incoming_sensitivity[0]
    doc_ends = jnp.cumsum(reply_list_sizes[0])[:-1]

    def doc_of(positions):
        return jnp.sum((positions[..., None] >= doc_ends).astype(jnp.int32), axis=-1)

    def select_rows(source, channel_count, dilation, offset):
        column = channel_count * channel_extent
        column_block = source[:, column : column + channel_extent]
        return column_block.reshape(tokens // dilation, dilation, channel_extent)[:, offset]

    def spread_rows(values_sel, dilation, offset):
        per_dev = tokens // dilation
        holder = jnp.zeros((per_dev, dilation, channel_extent), values_sel.dtype)
        return holder.at[:, offset].set(values_sel).reshape(tokens, channel_extent)

    top_span = min(2 ** (level_count - 1), seq_devices)
    bit_order = list(range(top_span.bit_length() - 1))
    gathered, level_bits, level_masks = ([], [], [])
    for level_idx in range(level_count):
        group_span, dilation, offset_zero = level_plan(level_idx, 0, seq_devices)
        nbits = group_span.bit_length() - 1
        own_bits = [bit_num for bit_num in bit_order if bit_num < nbits]
        masks_now = [0]
        for bit_num in own_bits:
            masks_now = masks_now + [entry ^ 1 << bit_num for entry in masks_now]
        level_bits.append(own_bits)
        level_masks.append(masks_now)
        key_heads, val_heads = ([], [])
        for head_idx in range(2):
            offset = level_plan(level_idx, head_idx, seq_devices)[2]
            key_heads.append(select_rows(keyed, 2 * level_idx + head_idx, dilation, offset))
            val_heads.append(select_rows(valued, 2 * level_idx + head_idx, dilation, offset))
        gathered.append(
            jnp.concatenate([jnp.concatenate(key_heads, 1), jnp.concatenate(val_heads, 1)], 0)
        )
    for level_id in range(level_count):
        for bit_num in level_bits[level_id]:
            current = gathered[level_id]
            gathered[level_id] = jnp.concatenate([current, partner(current, "seq", bit_num)], 0)
    out_cols, dq_cols, scale_terms, level_grads = ([], [], [], [])
    for level_id in range(level_count):
        group_span, dilation, offset_zero = level_plan(level_id, 0, seq_devices)
        per_dev = tokens // dilation
        arranged = gathered[level_id].reshape(group_span, 2, per_dev, 2 * channel_extent)
        all_keys = arranged[:, 0].reshape(group_span * per_dev, 2 * channel_extent)
        all_vals = arranged[:, 1].reshape(group_span * per_dev, 2 * channel_extent)
        sources = jnp.bitwise_xor(device_idx, jnp.array(level_masks[level_id], jnp.int32))
        key_grad_heads, val_grad_heads = ([], [])
        for head_idx in range(2):
            offset = level_plan(level_id, head_idx, seq_devices)[2]
            channel_count = 2 * level_id + head_idx
            local_idx = jnp.arange(per_dev, dtype=jnp.int32) * dilation + offset
            query_docs = doc_of(device_idx * tokens + local_idx)
            key_docs = doc_of((sources[:, None] * tokens + local_idx[None, :]).reshape(-1))
            allowed = query_docs[:, None] == key_docs[None, :]
            query_sel = select_rows(queries, channel_count, dilation, offset)
            up_sel = select_rows(upstream, channel_count, dilation, offset)
            key_sel = all_keys[:, head_idx * channel_extent : (head_idx + 1) * channel_extent]
            val_sel = all_vals[:, head_idx * channel_extent : (head_idx + 1) * channel_extent]
            raw = lax.dot_general(
                query_sel, key_sel, (((1,), (1,)), ((), ())), preferred_element_type=jnp.float32
            )
            logit_multiplier = learned_sharpness[channel_count] / math.sqrt(channel_extent)
            scores = jnp.where(allowed, raw * logit_multiplier, -jnp.inf)
            highest = jnp.max(scores, axis=1, keepdims=True)
            expo = jnp.where(allowed, jnp.exp(scores - highest), 0.0)
            probs = expo / jnp.sum(expo, axis=1, keepdims=True)
            probs_narrow = probs.astype(jnp.bfloat16)
            attended_output = jnp.dot(probs_narrow, val_sel, preferred_element_type=jnp.float32)
            delta = jnp.sum(up_sel.astype(jnp.float32) * attended_output, axis=1, keepdims=True)
            gradient_probs = lax.dot_general(
                up_sel, val_sel, (((1,), (1,)), ((), ())), preferred_element_type=jnp.float32
            )
            dscores = probs * (gradient_probs - delta)
            scale_terms.append(jnp.sum(dscores * raw) / math.sqrt(channel_extent))
            dscore_low = dscores.astype(jnp.bfloat16)
            grad_q = (
                jnp.dot(dscore_low, key_sel, preferred_element_type=jnp.float32) * logit_multiplier
            )
            grad_k = (
                lax.dot_general(
                    dscore_low,
                    query_sel,
                    (((0,), (0,)), ((), ())),
                    preferred_element_type=jnp.float32,
                )
                * logit_multiplier
            )
            grad_v = lax.dot_general(
                probs_narrow, up_sel, (((0,), (0,)), ((), ())), preferred_element_type=jnp.float32
            )
            out_cols.append(spread_rows(attended_output.astype(jnp.bfloat16), dilation, offset))
            dq_cols.append(spread_rows(grad_q.astype(jnp.bfloat16), dilation, offset))
            key_grad_heads.append(grad_k)
            val_grad_heads.append(grad_v)
        key_pack = jnp.concatenate(key_grad_heads, 1).reshape(
            group_span, per_dev, 2 * channel_extent
        )
        val_pack = jnp.concatenate(val_grad_heads, 1).reshape(
            group_span, per_dev, 2 * channel_extent
        )
        level_grads.append(
            jnp.stack([key_pack, val_pack], 1).reshape(group_span * 2 * per_dev, 2 * channel_extent)
        )
    for level_id in range(level_count):
        for bit_num in level_bits[level_id][::-1]:
            current = level_grads[level_id]
            half_rows = current.shape[0] // 2
            level_grads[level_id] = current[:half_rows] + partner(
                current[half_rows:], "seq", bit_num
            )
    dk_cols, dv_cols = ([], [])
    for level_id in range(level_count):
        group_span, dilation, offset_zero = level_plan(level_id, 0, seq_devices)
        per_dev = tokens // dilation
        own_grad = level_grads[level_id]
        for head_idx in range(2):
            offset = level_plan(level_id, head_idx, seq_devices)[2]
            cols_lo = head_idx * channel_extent
            key_part = own_grad[:per_dev, cols_lo : cols_lo + channel_extent]
            val_part = own_grad[per_dev:, cols_lo : cols_lo + channel_extent]
            dk_cols.append(spread_rows(key_part.astype(jnp.bfloat16), dilation, offset))
            dv_cols.append(spread_rows(val_part.astype(jnp.bfloat16), dilation, offset))
    scale_gradient = lax.psum(jnp.stack(scale_terms), ("seq", "dp"))
    attention_result = jnp.concatenate(out_cols, 1)[None]
    query_gradient = jnp.concatenate(dq_cols, 1)[None]
    key_gradient = jnp.concatenate(dk_cols, 1)[None]
    value_gradient = jnp.concatenate(dv_cols, 1)[None]
    return (attention_result, query_gradient, key_gradient, value_gradient, scale_gradient)


def solution(mesh):
    in_specs = (
        P("dp", "seq", None),
        P("dp", "seq", None),
        P("dp", "seq", None),
        P("dp", "seq", None),
        P(),
        P("dp", None),
    )
    out_specs = (
        P("dp", "seq", None),
        P("dp", "seq", None),
        P("dp", "seq", None),
        P("dp", "seq", None),
        P(),
    )
    return jax.shard_map(body, mesh=mesh, in_specs=in_specs, out_specs=out_specs, check_vma=False)
```

profile of v0, /device:TPU:4, one launch (start us, length us, event | category | flops | bytes accessed | tf_op | source)
XLA Modules:
  0.0 628.4 jit_solution(6130555929108911474)
XLA Ops:
  2.0 3.8 collective-permute-start.21
  5.9 2.0 collective-permute-start.15
  8.1 3.8 collective-permute-start.10
  12.1 2.0 collective-permute-start.6
  14.2 3.8 collective-permute-start.3
  59.5 2.0 collective-permute-start.1
  61.6 5.2 collective-permute-start.22
  68.4 3.8 collective-permute-start
  72.2 4.8 collective-permute-start.16
  78.7 9.1 %collective-permute-start.23 = (bf16[32,256]{1,0:T(8,128)(2,1)S(1)}, bf16[32,256]{1,0:T(8,128)(2,1)S(1)}, u32[]{:S(2)}, u32[]{:S(2)}) collective-permute-start(bf16[32,256]{1,0:T(8,128)(2,1)S(1)} %pad_maximum_fusion.36), channel_id=1, source_target_pairs={{0,16},{4,20},{8,24},{12,28},{16,0},{20,4},{24,8},{28,12},{32,48},... | collective-permute-start | bytes 49160 | tf_op jit(solution)/shard_map/ppermute | solution.py:11
  89.5 4.8 collective-permute-start.11
  94.4 7.8 %collective-permute-start.17 = (bf16[64,256]{1,0:T(8,128)(2,1)S(1)}, bf16[64,256]{1,0:T(8,128)(2,1)S(1)}, u32[]{:S(2)}, u32[]{:S(2)}) collective-permute-start(bf16[64,256]{1,0:T(8,128)(2,1)S(1)} %pad_maximum_fusion.32), channel_id=1, source_target_pairs={{0,16},{4,20},{8,24},{12,28},{16,0},{20,4},{24,8},{28,12},{32,48},... | collective-permute-start | bytes 98312 | tf_op jit(solution)/shard_map/ppermute | solution.py:11
  102.9 8.2 %collective-permute-start.24 = (bf16[64,256]{1,0:T(8,128)(2,1)S(1)}, bf16[64,256]{1,0:T(8,128)(2,1)S(1)}, u32[]{:S(2)}, u32[]{:S(2)}) collective-permute-start(bf16[64,256]{1,0:T(8,128)(2,1)S(1)} %concatenate.419), channel_id=1, source_target_pairs={{0,32},{4,36},{8,40},{12,44},{16,48},{20,52},{24,56},{28,60},{32,0... | collective-permute-start | bytes 98312 | tf_op jit(solution)/shard_map/ppermute | solution.py:11
  111.7 3.4 collective-permute-start.7
  117.5 3.7 collective-permute-start.12
  121.3 10.2 %collective-permute-start.18 = (bf16[128,256]{1,0:T(8,128)(2,1)}, bf16[128,256]{1,0:T(8,128)(2,1)S(1)}, u32[]{:S(2)}, u32[]{:S(2)}) collective-permute-start(bf16[128,256]{1,0:T(8,128)(2,1)} %get-tuple-element.952), channel_id=1, source_target_pairs={{0,32},{4,36},{8,40},{12,44},{16,48},{20,52},{24,56},{28,60},{32,0... | collective-permute-start | bytes 196616 | tf_op jit(solution)/shard_map/ppermute | solution.py:11
  132.1 3.5 collective-permute-start.25
  136.9 3.1 collective-permute-start.4
  140.7 4.2 collective-permute-start.8
  145.6 6.4 %collective-permute-start.13 = (bf16[256,256]{1,0:T(8,128)(2,1)}, bf16[256,256]{1,0:T(8,128)(2,1)}, u32[]{:S(2)}, u32[]{:S(2)}) collective-permute-start(bf16[256,256]{1,0:T(8,128)(2,1)} %get-tuple-element.938), channel_id=1, source_target_pairs={{0,32},{4,36},{8,40},{12,44},{16,48},{20,52},{24,56},{28,60},{32,0... | collective-permute-start | bytes 393224 | tf_op jit(solution)/shard_map/ppermute | solution.py:11
  152.0 3.6 concatenate.421
  155.7 3.1 collective-permute-start.19
  163.4 5.0 collective-permute-start.26
  168.5 2.8 collective-permute-start.2
  172.1 6.6 %collective-permute-start.5 = (bf16[512,256]{1,0:T(8,128)(2,1)}, bf16[512,256]{1,0:T(8,128)(2,1)}, u32[]{:S(2)}, u32[]{:S(2)}) collective-permute-start(bf16[512,256]{1,0:T(8,128)(2,1)} %pad_maximum_fusion.21), channel_id=1, source_target_pairs={{0,16},{4,20},{8,24},{12,28},{16,0},{20,4},{24,8},{28,12},{32,48},... | collective-permute-start | bytes 786440 | tf_op jit(solution)/shard_map/ppermute | solution.py:11
  180.3 7.2 %collective-permute-start.9 = (bf16[512,256]{1,0:T(8,128)(2,1)}, bf16[512,256]{1,0:T(8,128)(2,1)}, u32[]{:S(2)}, u32[]{:S(2)}) collective-permute-start(bf16[512,256]{1,0:T(8,128)(2,1)} %get-tuple-element.925), channel_id=1, source_target_pairs={{0,32},{4,36},{8,40},{12,44},{16,48},{20,52},{24,56},{28,60},{32,0... | collective-permute-start | bytes 786440 | tf_op jit(solution)/shard_map/ppermute | solution.py:11
  189.2 2.6 collective-permute-start.14
  193.4 3.7 collective-permute-start.20
  197.1 4.3 concatenate.422
  202.1 3.1 collective-permute-start.27
  237.2 2.6 collective-permute-start.29
  253.9 2.8 collective-permute-start.28
  277.4 7.0 %collective-permute-start.31 = (f32[512,256]{1,0:T(8,128)}, f32[512,256]{1,0:T(8,128)}, u32[]{:S(2)}, u32[]{:S(2)}) collective-permute-start(f32[512,256]{1,0:T(8,128)} %bitcast.190), channel_id=1, source_target_pairs={{0,16},{4,20},{8,24},{12,28},{16,0},{20,4},{24,8},{28,12},{32,48},... | collective-permute-start | bytes 1572872 | tf_op jit(solution)/shard_map/ppermute | solution.py:11
  305.9 6.2 collective-permute-start.34
  327.9 1.9 fusion.64
  336.0 4.0 collective-permute-start.38
  340.0 1.9 concatenate.423
  358.0 2.0 copy.616
  360.1 2.0 stack_reshape.62
  368.8 98.5 %psum.7 = f32[16]{0:T(128)} all-reduce(f32[16]{0:T(128)S(1)} %stack.99), channel_id=1, replica_groups=mesh['seq'=128,'dp'=4] {'seq','dp'}, use_global_device_ids=true, to_apply=%region_89.90 | all-reduce | flops 16 | bytes 128 | tf_op jit(solution)/shard_map/psum | solution.py:161
  472.5 2.0 copy.653
  474.5 2.0 copy.652
  476.6 3.1 collective-permute-start.43
  481.3 4.4 collective-permute-start.49
  486.9 4.0 collective-permute-start.30
  492.0 2.2 collective-permute-start.32
  495.3 6.1 collective-permute-start.35
  502.5 6.6 %collective-permute-start.39 = (f32[256,256]{1,0:T(8,128)S(1)}, f32[256,256]{1,0:T(8,128)S(1)}, u32[]{:S(2)}, u32[]{:S(2)}) collective-permute-start(f32[256,256]{1,0:T(8,128)S(1)} %slice.2481), channel_id=1, source_target_pairs={{0,32},{4,36},{8,40},{12,44},{16,48},{20,52},{24,56},{28,60},{32,0... | collective-permute-start | bytes 786440 | tf_op jit(solution)/shard_map/ppermute | solution.py:11
  509.3 3.4 collective-permute-start.44
  512.8 4.0 collective-permute-start.50
  517.5 8.3 %collective-permute-done.32 = f32[256,256]{1,0:T(8,128)S(1)} collective-permute-done((f32[256,256]{1,0:T(8,128)S(1)}, f32[256,256]{1,0:T(8,128)S(1)}, u32[]{:S(2)}, u32[]{:S(2)}) %collective-permute-start.32) | collective-permute-done | bytes 262176 | tf_op jit(solution)/shard_map/ppermute | solution.py:11
  527.8 19.5 %collective-permute-done.35 = f32[256,256]{1,0:T(8,128)S(1)} collective-permute-done((f32[256,256]{1,0:T(8,128)S(1)}, f32[256,256]{1,0:T(8,128)S(1)}, u32[]{:S(2)}, u32[]{:S(2)}) %collective-permute-start.35) | collective-permute-done | bytes 262176 | tf_op jit(solution)/shard_map/ppermute | solution.py:11
  551.4 7.9 %collective-permute-start.45 = (f32[128,256]{1,0:T(8,128)S(1)}, f32[128,256]{1,0:T(8,128)S(1)}, u32[]{:S(2)}, u32[]{:S(2)}) collective-permute-start(f32[128,256]{1,0:T(8,128)S(1)} %slice.2495), channel_id=1, source_target_pairs={{0,32},{4,36},{8,40},{12,44},{16,48},{20,52},{24,56},{28,60},{32,0... | collective-permute-start | bytes 393224 | tf_op jit(solution)/shard_map/ppermute | solution.py:11
  559.4 2.1 collective-permute-start.51
  562.5 7.4 %collective-permute-start.37 = (f32[64,256]{1,0:T(8,128)S(1)}, f32[64,256]{1,0:T(8,128)S(1)}, u32[]{:S(2)}, u32[]{:S(2)}) collective-permute-start(f32[64,256]{1,0:T(8,128)S(1)} %slice.2475), channel_id=1, source_target_pairs={{0,4},{4,0},{8,12},{12,8},{16,20},{20,16},{24,28},{28,24},{32,36},... | collective-permute-start | bytes 196616 | tf_op jit(solution)/shard_map/ppermute | solution.py:11
  569.9 5.5 collective-permute-done.40
  577.5 9.5 %collective-permute-start.46 = (f32[64,256]{1,0:T(8,128)S(1)}, f32[64,256]{1,0:T(8,128)S(1)}, u32[]{:S(2)}, u32[]{:S(2)}) collective-permute-start(f32[64,256]{1,0:T(8,128)S(1)} %slice.2497), channel_id=1, source_target_pairs={{0,16},{4,20},{8,24},{12,28},{16,0},{20,4},{24,8},{28,12},{32,48},... | collective-permute-start | bytes 196616 | tf_op jit(solution)/shard_map/ppermute | solution.py:11
  587.0 8.0 %collective-permute-start.52 = (f32[64,256]{1,0:T(8,128)S(1)}, f32[64,256]{1,0:T(8,128)S(1)}, u32[]{:S(2)}, u32[]{:S(2)}) collective-permute-start(f32[64,256]{1,0:T(8,128)S(1)} %slice.2511), channel_id=1, source_target_pairs={{0,32},{4,36},{8,40},{12,44},{16,48},{20,52},{24,56},{28,60},{32,0... | collective-permute-start | bytes 196616 | tf_op jit(solution)/shard_map/ppermute | solution.py:11
  595.8 1.9 collective-permute-start.42
  599.7 4.2 collective-permute-done.52
  603.9 2.6 collective-permute-start.53
  609.2 4.4 collective-permute-done.53
  616.3 3.9 collective-permute-done.54
  622.2 3.6 collective-permute-done.55
  (847 shorter events, 210.2 us)
Async XLA Ops:
  2.0 57.5 %collective-permute-start.21 = (bf16[8,256]{1,0:T(8,128)(2,1)S(1)}, bf16[8,256]{1,0:T(8,128)(2,1)S(1)}, u32[]{:S(2)}, u32[]{:S(2)}) collective-permute-start(bf16[8,256]{1,0:T(8,128)(2,1)S(1)} %maximum_maximum_fusion.4), channel_id=1, source_target_pairs={{0,4},{4,0},{8,12},{12,8},{16,20},{20,16},{24,28},{28,24},{32,36},... | collective-permute-start | bytes 12296 | tf_op jit(solution)/shard_map/ppermute | solution.py:11
  5.9 55.6 %collective-permute-start.15 = (bf16[16,256]{1,0:T(8,128)(2,1)S(1)}, bf16[16,256]{1,0:T(8,128)(2,1)S(1)}, u32[]{:S(2)}, u32[]{:S(2)}) collective-permute-start(bf16[16,256]{1,0:T(8,128)(2,1)S(1)} %maximum_maximum_fusion.3), channel_id=1, source_target_pairs={{0,4},{4,0},{8,12},{12,8},{16,20},{20,16},{24,28},{28,24},{32,36},... | collective-permute-start | bytes 24584 | tf_op jit(solution)/shard_map/ppermute | solution.py:11
  8.1 64.1 %collective-permute-start.10 = (bf16[32,256]{1,0:T(8,128)(2,1)S(1)}, bf16[32,256]{1,0:T(8,128)(2,1)S(1)}, u32[]{:S(2)}, u32[]{:S(2)}) collective-permute-start(bf16[32,256]{1,0:T(8,128)(2,1)S(1)} %maximum_maximum_fusion.2), channel_id=1, source_target_pairs={{0,4},{4,0},{8,12},{12,8},{16,20},{20,16},{24,28},{28,24},{32,36},... | collective-permute-start | bytes 49160 | tf_op jit(solution)/shard_map/ppermute | solution.py:11
  12.1 82.3 %collective-permute-start.6 = (bf16[64,256]{1,0:T(8,128)(2,1)S(1)}, bf16[64,256]{1,0:T(8,128)(2,1)S(1)}, u32[]{:S(2)}, u32[]{:S(2)}) collective-permute-start(bf16[64,256]{1,0:T(8,128)(2,1)S(1)} %maximum_maximum_fusion.1), channel_id=1, source_target_pairs={{0,4},{4,0},{8,12},{12,8},{16,20},{20,16},{24,28},{28,24},{32,36},... | collective-permute-start | bytes 98312 | tf_op jit(solution)/shard_map/ppermute | solution.py:11
  14.2 107.0 %collective-permute-start.3 = (bf16[128,256]{1,0:T(8,128)(2,1)S(1)}, bf16[128,256]{1,0:T(8,128)(2,1)S(1)}, u32[]{:S(2)}, u32[]{:S(2)}) collective-permute-start(bf16[128,256]{1,0:T(8,128)(2,1)S(1)} %maximum_maximum_fusion), channel_id=1, source_target_pairs={{0,4},{4,0},{8,12},{12,8},{16,20},{20,16},{24,28},{28,24},{32,36},... | collective-permute-start | bytes 196616 | tf_op jit(solution)/shard_map/ppermute | solution.py:11
  26.8 4.2 copy-start.52
  59.5 103.3 %collective-permute-start.1 = (bf16[256,256]{1,0:T(8,128)(2,1)S(1)}, bf16[256,256]{1,0:T(8,128)(2,1)S(1)}, u32[]{:S(2)}, u32[]{:S(2)}) collective-permute-start(bf16[256,256]{1,0:T(8,128)(2,1)S(1)} %pad_maximum_fusion.26), channel_id=1, source_target_pairs={{0,4},{4,0},{8,12},{12,8},{16,20},{20,16},{24,28},{28,24},{32,36},... | collective-permute-start | bytes 393224 | tf_op jit(solution)/shard_map/ppermute | solution.py:11
  61.6 6.8 %collective-permute-start.22 = (bf16[16,256]{1,0:T(8,128)(2,1)S(1)}, bf16[16,256]{1,0:T(8,128)(2,1)S(1)}, u32[]{:S(2)}, u32[]{:S(2)}) collective-permute-start(bf16[16,256]{1,0:T(8,128)(2,1)S(1)} %pad_maximum_fusion.39), channel_id=1, source_target_pairs={{0,8},{4,12},{8,0},{12,4},{16,24},{20,28},{24,16},{28,20},{32,40},... | collective-permute-start | bytes 24584 | tf_op jit(solution)/shard_map/ppermute | solution.py:11
  68.4 87.3 %collective-permute-start = (bf16[256,256]{1,0:T(8,128)(2,1)S(1)}, bf16[256,256]{1,0:T(8,128)(2,1)S(1)}, u32[]{:S(2)}, u32[]{:S(2)}) collective-permute-start(bf16[256,256]{1,0:T(8,128)(2,1)S(1)} %pad_maximum_fusion.25), channel_id=1, source_target_pairs={{0,4},{4,0},{8,12},{12,8},{16,20},{20,16},{24,28},{28,24},{32,36},... | collective-permute-start | bytes 393224 | tf_op jit(solution)/shard_map/ppermute | solution.py:11
  72.2 6.5 %collective-permute-start.16 = (bf16[32,256]{1,0:T(8,128)(2,1)S(1)}, bf16[32,256]{1,0:T(8,128)(2,1)S(1)}, u32[]{:S(2)}, u32[]{:S(2)}) collective-permute-start(bf16[32,256]{1,0:T(8,128)(2,1)S(1)} %pad_maximum_fusion.35), channel_id=1, source_target_pairs={{0,8},{4,12},{8,0},{12,4},{16,24},{20,28},{24,16},{28,20},{32,40},... | collective-permute-start | bytes 49160 | tf_op jit(solution)/shard_map/ppermute | solution.py:11
  78.7 10.8 %collective-permute-start.23 = (bf16[32,256]{1,0:T(8,128)(2,1)S(1)}, bf16[32,256]{1,0:T(8,128)(2,1)S(1)}, u32[]{:S(2)}, u32[]{:S(2)}) collective-permute-start(bf16[32,256]{1,0:T(8,128)(2,1)S(1)} %pad_maximum_fusion.36), channel_id=1, source_target_pairs={{0,16},{4,20},{8,24},{12,28},{16,0},{20,4},{24,8},{28,12},{32,48},... | collective-permute-start | bytes 49160 | tf_op jit(solution)/shard_map/ppermute | solution.py:11
  89.5 13.3 %collective-permute-start.11 = (bf16[64,256]{1,0:T(8,128)(2,1)S(1)}, bf16[64,256]{1,0:T(8,128)(2,1)S(1)}, u32[]{:S(2)}, u32[]{:S(2)}) collective-permute-start(bf16[64,256]{1,0:T(8,128)(2,1)S(1)} %pad_maximum_fusion.31), channel_id=1, source_target_pairs={{0,8},{4,12},{8,0},{12,4},{16,24},{20,28},{24,16},{28,20},{32,40},... | collective-permute-start | bytes 98312 | tf_op jit(solution)/shard_map/ppermute | solution.py:11
  94.4 17.4 %collective-permute-start.17 = (bf16[64,256]{1,0:T(8,128)(2,1)S(1)}, bf16[64,256]{1,0:T(8,128)(2,1)S(1)}, u32[]{:S(2)}, u32[]{:S(2)}) collective-permute-start(bf16[64,256]{1,0:T(8,128)(2,1)S(1)} %pad_maximum_fusion.32), channel_id=1, source_target_pairs={{0,16},{4,20},{8,24},{12,28},{16,0},{20,4},{24,8},{28,12},{32,48},... | collective-permute-start | bytes 98312 | tf_op jit(solution)/shard_map/ppermute | solution.py:11
  102.9 14.6 %collective-permute-start.24 = (bf16[64,256]{1,0:T(8,128)(2,1)S(1)}, bf16[64,256]{1,0:T(8,128)(2,1)S(1)}, u32[]{:S(2)}, u32[]{:S(2)}) collective-permute-start(bf16[64,256]{1,0:T(8,128)(2,1)S(1)} %concatenate.419), channel_id=1, source_target_pairs={{0,32},{4,36},{8,40},{12,44},{16,48},{20,52},{24,56},{28,60},{32,0... | collective-permute-start | bytes 98312 | tf_op jit(solution)/shard_map/ppermute | solution.py:11
  111.7 20.4 %collective-permute-start.7 = (bf16[128,256]{1,0:T(8,128)(2,1)S(1)}, bf16[128,256]{1,0:T(8,128)(2,1)S(1)}, u32[]{:S(2)}, u32[]{:S(2)}) collective-permute-start(bf16[128,256]{1,0:T(8,128)(2,1)S(1)} %pad_maximum_fusion.29), channel_id=1, source_target_pairs={{0,8},{4,12},{8,0},{12,4},{16,24},{20,28},{24,16},{28,20},{32,40},... | collective-permute-start | bytes 196616 | tf_op jit(solution)/shard_map/ppermute | solution.py:11
  117.5 19.4 %collective-permute-start.12 = (bf16[128,256]{1,0:T(8,128)(2,1)S(1)}, bf16[128,256]{1,0:T(8,128)(2,1)S(1)}, u32[]{:S(2)}, u32[]{:S(2)}) collective-permute-start(bf16[128,256]{1,0:T(8,128)(2,1)S(1)} %pad_maximum_fusion.30), channel_id=1, source_target_pairs={{0,16},{4,20},{8,24},{12,28},{16,0},{20,4},{24,8},{28,12},{32,48},... | collective-permute-start | bytes 196616 | tf_op jit(solution)/shard_map/ppermute | solution.py:11
  121.3 19.5 %collective-permute-start.18 = (bf16[128,256]{1,0:T(8,128)(2,1)}, bf16[128,256]{1,0:T(8,128)(2,1)S(1)}, u32[]{:S(2)}, u32[]{:S(2)}) collective-permute-start(bf16[128,256]{1,0:T(8,128)(2,1)} %get-tuple-element.952), channel_id=1, source_target_pairs={{0,32},{4,36},{8,40},{12,44},{16,48},{20,52},{24,56},{28,60},{32,0... | collective-permute-start | bytes 196616 | tf_op jit(solution)/shard_map/ppermute | solution.py:11
  132.1 13.5 %collective-permute-start.25 = (bf16[128,256]{1,0:T(8,128)(2,1)S(1)}, bf16[128,256]{1,0:T(8,128)(2,1)S(1)}, u32[]{:S(2)}, u32[]{:S(2)}) collective-permute-start(bf16[128,256]{1,0:T(8,128)(2,1)S(1)} %concatenate.420), channel_id=1, source_target_pairs={{0,64},{4,68},{8,72},{12,76},{16,80},{20,84},{24,88},{28,92},{32,9... | collective-permute-start | bytes 196616 | tf_op jit(solution)/shard_map/ppermute | solution.py:11
  136.9 31.5 %collective-permute-start.4 = (bf16[256,256]{1,0:T(8,128)(2,1)}, bf16[256,256]{1,0:T(8,128)(2,1)S(1)}, u32[]{:S(2)}, u32[]{:S(2)}) collective-permute-start(bf16[256,256]{1,0:T(8,128)(2,1)} %pad_maximum_fusion.27), channel_id=1, source_target_pairs={{0,8},{4,12},{8,0},{12,4},{16,24},{20,28},{24,16},{28,20},{32,40},... | collective-permute-start | bytes 393224 | tf_op jit(solution)/shard_map/ppermute | solution.py:11
  140.7 31.3 %collective-permute-start.8 = (bf16[256,256]{1,0:T(8,128)(2,1)}, bf16[256,256]{1,0:T(8,128)(2,1)}, u32[]{:S(2)}, u32[]{:S(2)}) collective-permute-start(bf16[256,256]{1,0:T(8,128)(2,1)} %pad_maximum_fusion.28), channel_id=1, source_target_pairs={{0,16},{4,20},{8,24},{12,28},{16,0},{20,4},{24,8},{28,12},{32,48},... | collective-permute-start | bytes 393224 | tf_op jit(solution)/shard_map/ppermute | solution.py:11
  145.6 34.8 %collective-permute-start.13 = (bf16[256,256]{1,0:T(8,128)(2,1)}, bf16[256,256]{1,0:T(8,128)(2,1)}, u32[]{:S(2)}, u32[]{:S(2)}) collective-permute-start(bf16[256,256]{1,0:T(8,128)(2,1)} %get-tuple-element.938), channel_id=1, source_target_pairs={{0,32},{4,36},{8,40},{12,44},{16,48},{20,52},{24,56},{28,60},{32,0... | collective-permute-start | bytes 393224 | tf_op jit(solution)/shard_map/ppermute | solution.py:11
  155.7 33.5 %collective-permute-start.19 = (bf16[256,256]{1,0:T(8,128)(2,1)}, bf16[256,256]{1,0:T(8,128)(2,1)}, u32[]{:S(2)}, u32[]{:S(2)}) collective-permute-start(bf16[256,256]{1,0:T(8,128)(2,1)} %get-tuple-element.935), channel_id=1, source_target_pairs={{0,64},{4,68},{8,72},{12,76},{16,80},{20,84},{24,88},{28,92},{32,9... | collective-permute-start | bytes 393224 | tf_op jit(solution)/shard_map/ppermute | solution.py:11
  163.4 30.0 %collective-permute-start.26 = (bf16[256,256]{1,0:T(8,128)(2,1)S(1)}, bf16[256,256]{1,0:T(8,128)(2,1)S(1)}, u32[]{:S(2)}, u32[]{:S(2)}) collective-permute-start(bf16[256,256]{1,0:T(8,128)(2,1)S(1)} %copy-done.25), channel_id=1, source_target_pairs={{0,128},{4,132},{8,136},{12,140},{16,144},{20,148},{24,152},{28,15... | collective-permute-start | bytes 393224 | tf_op jit(solution)/shard_map/ppermute | solution.py:11
  168.5 33.0 %collective-permute-start.2 = (bf16[512,256]{1,0:T(8,128)(2,1)S(1)}, bf16[512,256]{1,0:T(8,128)(2,1)S(1)}, u32[]{:S(2)}, u32[]{:S(2)}) collective-permute-start(bf16[512,256]{1,0:T(8,128)(2,1)S(1)} %pad_maximum_fusion.20), channel_id=1, source_target_pairs={{0,8},{4,12},{8,0},{12,4},{16,24},{20,28},{24,16},{28,20},{32,40},... | collective-permute-start | bytes 786440 | tf_op jit(solution)/shard_map/ppermute | solution.py:11
  172.1 65.1 %collective-permute-start.5 = (bf16[512,256]{1,0:T(8,128)(2,1)}, bf16[512,256]{1,0:T(8,128)(2,1)}, u32[]{:S(2)}, u32[]{:S(2)}) collective-permute-start(bf16[512,256]{1,0:T(8,128)(2,1)} %pad_maximum_fusion.21), channel_id=1, source_target_pairs={{0,16},{4,20},{8,24},{12,28},{16,0},{20,4},{24,8},{28,12},{32,48},... | collective-permute-start | bytes 786440 | tf_op jit(solution)/shard_map/ppermute | solution.py:11
  180.3 73.6 %collective-permute-start.9 = (bf16[512,256]{1,0:T(8,128)(2,1)}, bf16[512,256]{1,0:T(8,128)(2,1)}, u32[]{:S(2)}, u32[]{:S(2)}) collective-permute-start(bf16[512,256]{1,0:T(8,128)(2,1)} %get-tuple-element.925), channel_id=1, source_target_pairs={{0,32},{4,36},{8,40},{12,44},{16,48},{20,52},{24,56},{28,60},{32,0... | collective-permute-start | bytes 786440 | tf_op jit(solution)/shard_map/ppermute | solution.py:11
  189.2 88.2 %collective-permute-start.14 = (bf16[512,256]{1,0:T(8,128)(2,1)}, bf16[512,256]{1,0:T(8,128)(2,1)}, u32[]{:S(2)}, u32[]{:S(2)}) collective-permute-start(bf16[512,256]{1,0:T(8,128)(2,1)} %get-tuple-element.923), channel_id=1, source_target_pairs={{0,64},{4,68},{8,72},{12,76},{16,80},{20,84},{24,88},{28,92},{32,9... | collective-permute-start | bytes 786440 | tf_op jit(solution)/shard_map/ppermute | solution.py:11
  193.4 8.0 %copy-start.9 = (bf16[256,256]{1,0:T(8,128)(2,1)}, bf16[256,256]{1,0:T(8,128)(2,1)S(1)}, u32[]{:S(2)}) copy-start(bf16[256,256]{1,0:T(8,128)(2,1)S(1)} %collective-permute-done.26) | copy-start | bytes 393220
  193.4 112.5 %collective-permute-start.20 = (bf16[512,256]{1,0:T(8,128)(2,1)}, bf16[512,256]{1,0:T(8,128)(2,1)}, u32[]{:S(2)}, u32[]{:S(2)}) collective-permute-start(bf16[512,256]{1,0:T(8,128)(2,1)} %get-tuple-element.921), channel_id=1, source_target_pairs={{0,128},{4,132},{8,136},{12,140},{16,144},{20,148},{24,152},{28,15... | collective-permute-start | bytes 786440 | tf_op jit(solution)/shard_map/ppermute | solution.py:11
  202.1 133.9 %collective-permute-start.27 = (bf16[512,256]{1,0:T(8,128)(2,1)}, bf16[512,256]{1,0:T(8,128)(2,1)}, u32[]{:S(2)}, u32[]{:S(2)}) collective-permute-start(bf16[512,256]{1,0:T(8,128)(2,1)} %concatenate.422), channel_id=1, source_target_pairs={{0,256},{4,260},{8,264},{12,268},{16,272},{20,276},{24,280},{28,28... | collective-permute-start | bytes 786440 | tf_op jit(solution)/shard_map/ppermute | solution.py:11
  206.3 21.2 %copy-start.5 = (bf16[4,1,128,256]{3,2,1,0:T(8,128)(2,1)}, bf16[4,1,128,256]{3,2,1,0:T(8,128)(2,1)S(1)}, u32[]{:S(2)}) copy-start(bf16[4,1,128,256]{3,2,1,0:T(8,128)(2,1)S(1)} %get-tuple-element.905) | copy-start | bytes 786436
  214.3 5.9 copy-start.36
  215.1 5.3 copy-start.38
  216.7 4.4 copy-start.46
  237.2 244.1 %collective-permute-start.29 = (f32[512,256]{0,1:T(8,128)}, f32[512,256]{0,1:T(8,128)}, u32[]{:S(2)}, u32[]{:S(2)}) collective-permute-start(f32[512,256]{0,1:T(8,128)} %slice.2212), channel_id=1, source_target_pairs={{0,8},{4,12},{8,0},{12,4},{16,24},{20,28},{24,16},{28,20},{32,40},... | collective-permute-start | bytes 1572872 | tf_op jit(solution)/shard_map/ppermute | solution.py:11
  253.9 222.6 %collective-permute-start.28 = (f32[256,256]{0,1:T(8,128)}, f32[256,256]{0,1:T(8,128)}, u32[]{:S(2)}, u32[]{:S(2)}) collective-permute-start(f32[256,256]{0,1:T(8,128)} %bitcast.622), channel_id=1, source_target_pairs={{0,4},{4,0},{8,12},{12,8},{16,20},{20,16},{24,28},{28,24},{32,36},... | collective-permute-start | bytes 786440 | tf_op jit(solution)/shard_map/ppermute | solution.py:11
  277.4 209.5 %collective-permute-start.31 = (f32[512,256]{1,0:T(8,128)}, f32[512,256]{1,0:T(8,128)}, u32[]{:S(2)}, u32[]{:S(2)}) collective-permute-start(f32[512,256]{1,0:T(8,128)} %bitcast.190), channel_id=1, source_target_pairs={{0,16},{4,20},{8,24},{12,28},{16,0},{20,4},{24,8},{28,12},{32,48},... | collective-permute-start | bytes 1572872 | tf_op jit(solution)/shard_map/ppermute | solution.py:11
  305.9 186.0 %collective-permute-start.34 = (f32[512,256]{1,0:T(8,128)}, f32[512,256]{1,0:T(8,128)}, u32[]{:S(2)}, u32[]{:S(2)}) collective-permute-start(f32[512,256]{1,0:T(8,128)} %bitcast.198), channel_id=1, source_target_pairs={{0,32},{4,36},{8,40},{12,44},{16,48},{20,52},{24,56},{28,60},{32,0... | collective-permute-start | bytes 1572872 | tf_op jit(solution)/shard_map/ppermute | solution.py:11
  313.8 3.8 copy-start.69
  336.0 159.3 %collective-permute-start.38 = (f32[512,256]{1,0:T(8,128)}, f32[512,256]{1,0:T(8,128)}, u32[]{:S(2)}, u32[]{:S(2)}) collective-permute-start(f32[512,256]{1,0:T(8,128)} %bitcast.206), channel_id=1, source_target_pairs={{0,64},{4,68},{8,72},{12,76},{16,80},{20,84},{24,88},{28,92},{32,9... | collective-permute-start | bytes 1572872 | tf_op jit(solution)/shard_map/ppermute | solution.py:11
  476.6 4.8 copy-start.8
  476.6 26.0 %collective-permute-start.43 = (f32[512,256]{1,0:T(8,128)}, f32[512,256]{1,0:T(8,128)S(1)}, u32[]{:S(2)}, u32[]{:S(2)}) collective-permute-start(f32[512,256]{1,0:T(8,128)} %bitcast.691), channel_id=1, source_target_pairs={{0,128},{4,132},{8,136},{12,140},{16,144},{20,148},{24,152},{28,15... | collective-permute-start | bytes 1572872 | tf_op jit(solution)/shard_map/ppermute | solution.py:11
  481.3 28.0 %collective-permute-start.49 = (f32[512,256]{1,0:T(8,128)S(1)}, f32[512,256]{1,0:T(8,128)S(1)}, u32[]{:S(2)}, u32[]{:S(2)}) collective-permute-start(f32[512,256]{1,0:T(8,128)S(1)} %copy-done.8), channel_id=1, source_target_pairs={{0,256},{4,260},{8,264},{12,268},{16,272},{20,276},{24,280},{28,28... | collective-permute-start | bytes 1572872 | tf_op jit(solution)/shard_map/ppermute | solution.py:11
  486.9 25.9 %collective-permute-start.30 = (f32[256,256]{0,1:T(8,128)S(1)}, f32[256,256]{0,1:T(8,128)S(1)}, u32[]{:S(2)}, u32[]{:S(2)}) collective-permute-start(f32[256,256]{0,1:T(8,128)S(1)} %slice.2458), channel_id=1, source_target_pairs={{0,4},{4,0},{8,12},{12,8},{16,20},{20,16},{24,28},{28,24},{32,36},... | collective-permute-start | bytes 786440 | tf_op jit(solution)/shard_map/ppermute | solution.py:11
  492.0 33.9 %collective-permute-start.32 = (f32[256,256]{1,0:T(8,128)S(1)}, f32[256,256]{1,0:T(8,128)S(1)}, u32[]{:S(2)}, u32[]{:S(2)}) collective-permute-start(f32[256,256]{1,0:T(8,128)S(1)} %slice.2463), channel_id=1, source_target_pairs={{0,8},{4,12},{8,0},{12,4},{16,24},{20,28},{24,16},{28,20},{32,40},... | collective-permute-start | bytes 786440 | tf_op jit(solution)/shard_map/ppermute | solution.py:11
  495.3 52.0 %collective-permute-start.35 = (f32[256,256]{1,0:T(8,128)S(1)}, f32[256,256]{1,0:T(8,128)S(1)}, u32[]{:S(2)}, u32[]{:S(2)}) collective-permute-start(f32[256,256]{1,0:T(8,128)S(1)} %slice.2471), channel_id=1, source_target_pairs={{0,16},{4,20},{8,24},{12,28},{16,0},{20,4},{24,8},{28,12},{32,48},... | collective-permute-start | bytes 786440 | tf_op jit(solution)/shard_map/ppermute | solution.py:11
  502.5 46.8 %collective-permute-start.39 = (f32[256,256]{1,0:T(8,128)S(1)}, f32[256,256]{1,0:T(8,128)S(1)}, u32[]{:S(2)}, u32[]{:S(2)}) collective-permute-start(f32[256,256]{1,0:T(8,128)S(1)} %slice.2481), channel_id=1, source_target_pairs={{0,32},{4,36},{8,40},{12,44},{16,48},{20,52},{24,56},{28,60},{32,0... | collective-permute-start | bytes 786440 | tf_op jit(solution)/shard_map/ppermute | solution.py:11
  509.3 42.0 %collective-permute-start.44 = (f32[256,256]{1,0:T(8,128)S(1)}, f32[256,256]{1,0:T(8,128)S(1)}, u32[]{:S(2)}, u32[]{:S(2)}) collective-permute-start(f32[256,256]{1,0:T(8,128)S(1)} %slice.2493), channel_id=1, source_target_pairs={{0,64},{4,68},{8,72},{12,76},{16,80},{20,84},{24,88},{28,92},{32,9... | collective-permute-start | bytes 786440 | tf_op jit(solution)/shard_map/ppermute | solution.py:11
  512.8 46.5 %collective-permute-start.50 = (f32[256,256]{1,0:T(8,128)S(1)}, f32[256,256]{1,0:T(8,128)S(1)}, u32[]{:S(2)}, u32[]{:S(2)}) collective-permute-start(f32[256,256]{1,0:T(8,128)S(1)} %slice.2507), channel_id=1, source_target_pairs={{0,128},{4,132},{8,136},{12,140},{16,144},{20,148},{24,152},{28,15... | collective-permute-start | bytes 786440 | tf_op jit(solution)/shard_map/ppermute | solution.py:11
  525.9 35.6 %collective-permute-start.33 = (f32[128,256]{1,0:T(8,128)S(1)}, f32[128,256]{1,0:T(8,128)S(1)}, u32[]{:S(2)}, u32[]{:S(2)}) collective-permute-start(f32[128,256]{1,0:T(8,128)S(1)} %slice.2465), channel_id=1, source_target_pairs={{0,4},{4,0},{8,12},{12,8},{16,20},{20,16},{24,28},{28,24},{32,36},... | collective-permute-start | bytes 393224 | tf_op jit(solution)/shard_map/ppermute | solution.py:11
  547.4 15.1 %collective-permute-start.36 = (f32[128,256]{1,0:T(8,128)S(1)}, f32[128,256]{1,0:T(8,128)S(1)}, u32[]{:S(2)}, u32[]{:S(2)}) collective-permute-start(f32[128,256]{1,0:T(8,128)S(1)} %slice.2473), channel_id=1, source_target_pairs={{0,8},{4,12},{8,0},{12,4},{16,24},{20,28},{24,16},{28,20},{32,40},... | collective-permute-start | bytes 393224 | tf_op jit(solution)/shard_map/ppermute | solution.py:11
  549.4 26.1 %collective-permute-start.40 = (f32[128,256]{1,0:T(8,128)S(1)}, f32[128,256]{1,0:T(8,128)S(1)}, u32[]{:S(2)}, u32[]{:S(2)}) collective-permute-start(f32[128,256]{1,0:T(8,128)S(1)} %slice.2483), channel_id=1, source_target_pairs={{0,16},{4,20},{8,24},{12,28},{16,0},{20,4},{24,8},{28,12},{32,48},... | collective-permute-start | bytes 393224 | tf_op jit(solution)/shard_map/ppermute | solution.py:11
  551.4 26.1 %collective-permute-start.45 = (f32[128,256]{1,0:T(8,128)S(1)}, f32[128,256]{1,0:T(8,128)S(1)}, u32[]{:S(2)}, u32[]{:S(2)}) collective-permute-start(f32[128,256]{1,0:T(8,128)S(1)} %slice.2495), channel_id=1, source_target_pairs={{0,32},{4,36},{8,40},{12,44},{16,48},{20,52},{24,56},{28,60},{32,0... | collective-permute-start | bytes 393224 | tf_op jit(solution)/shard_map/ppermute | solution.py:11
  559.4 27.5 %collective-permute-start.51 = (f32[128,256]{1,0:T(8,128)S(1)}, f32[128,256]{1,0:T(8,128)S(1)}, u32[]{:S(2)}, u32[]{:S(2)}) collective-permute-start(f32[128,256]{1,0:T(8,128)S(1)} %slice.2509), channel_id=1, source_target_pairs={{0,64},{4,68},{8,72},{12,76},{16,80},{20,84},{24,88},{28,92},{32,9... | collective-permute-start | bytes 393224 | tf_op jit(solution)/shard_map/ppermute | solution.py:11
  562.5 32.5 %collective-permute-start.37 = (f32[64,256]{1,0:T(8,128)S(1)}, f32[64,256]{1,0:T(8,128)S(1)}, u32[]{:S(2)}, u32[]{:S(2)}) collective-permute-start(f32[64,256]{1,0:T(8,128)S(1)} %slice.2475), channel_id=1, source_target_pairs={{0,4},{4,0},{8,12},{12,8},{16,20},{20,16},{24,28},{28,24},{32,36},... | collective-permute-start | bytes 196616 | tf_op jit(solution)/shard_map/ppermute | solution.py:11
  575.5 20.3 %collective-permute-start.41 = (f32[64,256]{1,0:T(8,128)S(1)}, f32[64,256]{1,0:T(8,128)S(1)}, u32[]{:S(2)}, u32[]{:S(2)}) collective-permute-start(f32[64,256]{1,0:T(8,128)S(1)} %slice.2485), channel_id=1, source_target_pairs={{0,8},{4,12},{8,0},{12,4},{16,24},{20,28},{24,16},{28,20},{32,40},... | collective-permute-start | bytes 196616 | tf_op jit(solution)/shard_map/ppermute | solution.py:11
  577.5 20.3 %collective-permute-start.46 = (f32[64,256]{1,0:T(8,128)S(1)}, f32[64,256]{1,0:T(8,128)S(1)}, u32[]{:S(2)}, u32[]{:S(2)}) collective-permute-start(f32[64,256]{1,0:T(8,128)S(1)} %slice.2497), channel_id=1, source_target_pairs={{0,16},{4,20},{8,24},{12,28},{16,0},{20,4},{24,8},{28,12},{32,48},... | collective-permute-start | bytes 196616 | tf_op jit(solution)/shard_map/ppermute | solution.py:11
  587.0 16.9 %collective-permute-start.52 = (f32[64,256]{1,0:T(8,128)S(1)}, f32[64,256]{1,0:T(8,128)S(1)}, u32[]{:S(2)}, u32[]{:S(2)}) collective-permute-start(f32[64,256]{1,0:T(8,128)S(1)} %slice.2511), channel_id=1, source_target_pairs={{0,32},{4,36},{8,40},{12,44},{16,48},{20,52},{24,56},{28,60},{32,0... | collective-permute-start | bytes 196616 | tf_op jit(solution)/shard_map/ppermute | solution.py:11
  595.8 10.7 %collective-permute-start.42 = (f32[32,256]{1,0:T(8,128)S(1)}, f32[32,256]{1,0:T(8,128)S(1)}, u32[]{:S(2)}, u32[]{:S(2)}) collective-permute-start(f32[32,256]{1,0:T(8,128)S(1)} %slice.2487), channel_id=1, source_target_pairs={{0,4},{4,0},{8,12},{12,8},{16,20},{20,16},{24,28},{28,24},{32,36},... | collective-permute-start | bytes 98312 | tf_op jit(solution)/shard_map/ppermute | solution.py:11
  597.8 9.5 %collective-permute-start.47 = (f32[32,256]{1,0:T(8,128)S(1)}, f32[32,256]{1,0:T(8,128)S(1)}, u32[]{:S(2)}, u32[]{:S(2)}) collective-permute-start(f32[32,256]{1,0:T(8,128)S(1)} %slice.2499), channel_id=1, source_target_pairs={{0,8},{4,12},{8,0},{12,4},{16,24},{20,28},{24,16},{28,20},{32,40},... | collective-permute-start | bytes 98312 | tf_op jit(solution)/shard_map/ppermute | solution.py:11
  603.9 9.7 %collective-permute-start.53 = (f32[32,256]{1,0:T(8,128)S(1)}, f32[32,256]{1,0:T(8,128)S(1)}, u32[]{:S(2)}, u32[]{:S(2)}) collective-permute-start(f32[32,256]{1,0:T(8,128)S(1)} %slice.2513), channel_id=1, source_target_pairs={{0,16},{4,20},{8,24},{12,28},{16,0},{20,4},{24,8},{28,12},{32,48},... | collective-permute-start | bytes 98312 | tf_op jit(solution)/shard_map/ppermute | solution.py:11
  607.3 8.3 %collective-permute-start.48 = (f32[16,256]{1,0:T(8,128)S(1)}, f32[16,256]{1,0:T(8,128)S(1)}, u32[]{:S(2)}, u32[]{:S(2)}) collective-permute-start(f32[16,256]{1,0:T(8,128)S(1)} %slice.2501), channel_id=1, source_target_pairs={{0,4},{4,0},{8,12},{12,8},{16,20},{20,16},{24,28},{28,24},{32,36},... | collective-permute-start | bytes 49160 | tf_op jit(solution)/shard_map/ppermute | solution.py:11
  613.7 6.5 %collective-permute-start.54 = (f32[16,256]{1,0:T(8,128)S(1)}, f32[16,256]{1,0:T(8,128)S(1)}, u32[]{:S(2)}, u32[]{:S(2)}) collective-permute-start(f32[16,256]{1,0:T(8,128)S(1)} %slice.2515), channel_id=1, source_target_pairs={{0,8},{4,12},{8,0},{12,4},{16,24},{20,28},{24,16},{28,20},{32,40},... | collective-permute-start | bytes 49160 | tf_op jit(solution)/shard_map/ppermute | solution.py:11
  620.2 5.5 collective-permute-start.55
  (109 other events, 119.7 us)
where the time goes:
time: 634 us; the launch traced here: 628 us
  starting transfers between devices  241 us (38%)
  local copies, waits for them, and re-layouts  133 us (21%)
  blocking collectives  98.5 us (16%)
  waiting for transfers between devices  54.5 us (9%)
  matrix products  47.1 us (7%)
  other arithmetic  29.4 us (5%)
  between operations  24.8 us (4%)
    ppermute x56, starting transfers between devices, partner(): lax.ppermute(array, axis, [(i, i ^ 1 << apart) for i in range(lax.axis_si...  241 us
    psum x1, blocking collectives, body(): scale_gradient = lax.psum(jnp.stack(scale_terms), ('seq', 'dp'))  98.5 us
    ppermute x56, waiting for transfers between devices, partner(): lax.ppermute(array, axis, [(i, i ^ 1 << apart) for i in range(lax.axis_si...  54.5 us
    unnamed x331, local copies, waits for them, and re-layouts  54 us
    concatenate x12, local copies, waits for them, and re-layouts, body(): jnp.concatenate([current, partner(current, 'seq', bit_num)], 0)  20.7 us
    dot_general x16, matrix products, body(): lax.dot_general(up_sel, val_sel, (((1,), (1,)), ((), ())), preferred_elem...  13.5 us
  transfers between devices with their start and end apart: 56, of which 11 were waited for; matrix products, arithmetic and copies ran while one was open for 29% of the time, Pallas kernels for 0%

commit v1 on v0

--- a/solution.py
+++ b/solution.py
@@ -158,7 +158,7 @@
             val_part = own_grad[per_dev:, cols_lo : cols_lo + channel_extent]
             dk_cols.append(spread_rows(key_part.astype(jnp.bfloat16), dilation, offset))
             dv_cols.append(spread_rows(val_part.astype(jnp.bfloat16), dilation, offset))
-    scale_gradient = lax.psum(jnp.stack(scale_terms), ("seq", "dp"))
+    scale_gradient = jnp.sum(lax.all_gather(jnp.stack(scale_terms), ("seq", "dp")), axis=0)
     attention_result = jnp.concatenate(out_cols, 1)[None]
     query_gradient = jnp.concatenate(dq_cols, 1)[None]
     key_gradient = jnp.concatenate(dk_cols, 1)[None]

time: 634 us -> 653 us (1.030)
  other arithmetic: 29.4 us -> 41.2 us
  local copies, waits for them, and re-layouts: 133 us -> 141 us
    unnamed x0 -> x1, blocking collectives: none -> 99.4 us
    psum x1 -> x0, blocking collectives: 98.5 us -> none  [body(): scale_gradient = lax.psum(jnp.stack(scale_terms), ('seq', 'dp'))]
    unnamed x331 -> x429, local copies, waits for them, and re-layouts: 54 us -> 58.2 us
  transfers between devices with their start and end apart: 56 -> 56, of which waited for: 11 -> 10; matrix products, arithmetic and copies ran while one was open for 29% -> 30% of each run, Pallas kernels for 0% -> 0%
where the time goes in v1:
time: 653 us; the launch traced here: 648 us
  starting transfers between devices  242 us (37%)
  local copies, waits for them, and re-layouts  141 us (22%)
  blocking collectives  99.4 us (15%)
  waiting for transfers between devices  50.8 us (8%)
  matrix products  48.8 us (7%)
  other arithmetic  41.2 us (6%)
  between operations  25.1 us (4%)
    ppermute x56, starting transfers between devices, partner(): lax.ppermute(array, axis, [(i, i ^ 1 << apart) for i in range(lax.axis_si...  242 us
    unnamed x1, blocking collectives  99.4 us
    unnamed x429, local copies, waits for them, and re-layouts  58.2 us
    ppermute x56, waiting for transfers between devices, partner(): lax.ppermute(array, axis, [(i, i ^ 1 << apart) for i in range(lax.axis_si...  50.8 us
    concatenate x12, local copies, waits for them, and re-layouts, body(): jnp.concatenate([current, partner(current, 'seq', bit_num)], 0)  18.7 us
    slice x36, local copies, waits for them, and re-layouts, select_rows(): column_block.reshape(tokens // dilation, dilation, channel_extent)  14.1 us
    dot_general x16, matrix products, body(): lax.dot_general(up_sel, val_sel, (((1,), (1,)), ((), ())), preferred_elem...  13.9 us
  transfers between devices with their start and end apart: 56, of which 10 were waited for; matrix products, arithmetic and copies ran while one was open for 30% of the time, Pallas kernels for 0%

profile of v1, /device:TPU:4, one launch (start us, length us, event | category | flops | bytes accessed | tf_op | source)
XLA Modules:
  0.0 647.7 jit_solution(17001866790490246314)
XLA Ops:
  2.6 3.8 collective-permute-start.21
  7.7 2.0 collective-permute-start.15
  10.5 3.8 collective-permute-start.10
  15.0 2.0 collective-permute-start.6
  17.8 3.8 collective-permute-start.3
  80.0 2.0 collective-permute-start.1
  82.1 5.2 collective-permute-start.22
  89.3 3.8 collective-permute-start
  93.2 4.4 collective-permute-start.16
  99.7 9.1 %collective-permute-start.23 = (bf16[32,256]{1,0:T(8,128)(2,1)S(1)}, bf16[32,256]{1,0:T(8,128)(2,1)S(1)}, u32[]{:S(2)}, u32[]{:S(2)}) collective-permute-start(bf16[32,256]{1,0:T(8,128)(2,1)S(1)} %pad_maximum_fusion.36), channel_id=1, source_target_pairs={{0,16},{4,20},{8,24},{12,28},{16,0},{20,4},{24,8},{28,12},{32,48},... | collective-permute-start | bytes 49160 | tf_op jit(solution)/shard_map/ppermute | solution.py:11
  110.5 4.4 collective-permute-start.11
  114.9 7.9 %collective-permute-start.17 = (bf16[64,256]{1,0:T(8,128)(2,1)S(1)}, bf16[64,256]{1,0:T(8,128)(2,1)S(1)}, u32[]{:S(2)}, u32[]{:S(2)}) collective-permute-start(bf16[64,256]{1,0:T(8,128)(2,1)S(1)} %pad_maximum_fusion.32), channel_id=1, source_target_pairs={{0,16},{4,20},{8,24},{12,28},{16,0},{20,4},{24,8},{28,12},{32,48},... | collective-permute-start | bytes 98312 | tf_op jit(solution)/shard_map/ppermute | solution.py:11
  123.5 8.1 %collective-permute-start.24 = (bf16[64,256]{1,0:T(8,128)(2,1)S(1)}, bf16[64,256]{1,0:T(8,128)(2,1)S(1)}, u32[]{:S(2)}, u32[]{:S(2)}) collective-permute-start(bf16[64,256]{1,0:T(8,128)(2,1)S(1)} %concatenate.419), channel_id=1, source_target_pairs={{0,32},{4,36},{8,40},{12,44},{16,48},{20,52},{24,56},{28,60},{32,0... | collective-permute-start | bytes 98312 | tf_op jit(solution)/shard_map/ppermute | solution.py:11
  132.3 3.4 collective-permute-start.7
  138.1 3.7 collective-permute-start.12
  141.8 10.2 %collective-permute-start.18 = (bf16[128,256]{1,0:T(8,128)(2,1)}, bf16[128,256]{1,0:T(8,128)(2,1)S(1)}, u32[]{:S(2)}, u32[]{:S(2)}) collective-permute-start(bf16[128,256]{1,0:T(8,128)(2,1)} %get-tuple-element.952), channel_id=1, source_target_pairs={{0,32},{4,36},{8,40},{12,44},{16,48},{20,52},{24,56},{28,60},{32,0... | collective-permute-start | bytes 196616 | tf_op jit(solution)/shard_map/ppermute | solution.py:11
  152.7 3.5 collective-permute-start.25
  157.5 3.0 collective-permute-start.4
  161.2 4.2 collective-permute-start.8
  166.2 6.2 collective-permute-start.13
  172.3 3.6 concatenate.421
  176.0 3.6 collective-permute-start.19
  184.4 4.9 collective-permute-start.26
  190.2 2.9 collective-permute-start.2
  193.9 6.4 collective-permute-start.5
  201.8 7.3 %collective-permute-start.9 = (bf16[512,256]{1,0:T(8,128)(2,1)}, bf16[512,256]{1,0:T(8,128)(2,1)}, u32[]{:S(2)}, u32[]{:S(2)}) collective-permute-start(bf16[512,256]{1,0:T(8,128)(2,1)} %get-tuple-element.925), channel_id=1, source_target_pairs={{0,32},{4,36},{8,40},{12,44},{16,48},{20,52},{24,56},{28,60},{32,0... | collective-permute-start | bytes 786440 | tf_op jit(solution)/shard_map/ppermute | solution.py:11
  210.7 2.6 collective-permute-start.14
  215.0 3.7 collective-permute-start.20
  218.7 4.3 concatenate.422
  223.1 2.8 collective-permute-start.27
  258.6 2.8 collective-permute-start.29
  275.6 2.9 collective-permute-start.28
  297.4 6.6 %collective-permute-start.31 = (f32[512,256]{1,0:T(8,128)}, f32[512,256]{1,0:T(8,128)}, u32[]{:S(2)}, u32[]{:S(2)}) collective-permute-start(f32[512,256]{1,0:T(8,128)} %bitcast.190), channel_id=1, source_target_pairs={{0,16},{4,20},{8,24},{12,28},{16,0},{20,4},{24,8},{28,12},{32,48},... | collective-permute-start | bytes 1572872 | tf_op jit(solution)/shard_map/ppermute | solution.py:11
  324.6 5.6 collective-permute-start.34
  344.8 1.9 fusion.64
  352.8 4.3 collective-permute-start.38
  357.1 1.9 concatenate.423
  375.2 2.0 copy.616
  377.2 2.0 stack_reshape.62
  386.3 99.4 %all-reduce.40 = f32[8192]{0:T(1024)S(1)} all-reduce(f32[8192]{0:T(1024)S(1)} %dynamic-update-slice.168), channel_id=2, replica_groups=mesh['seq'=128,'dp'=4] {'seq','dp'}, use_global_device_ids=true, to_apply=%add.40 | all-reduce | flops 8192 | bytes 65536
  491.6 2.0 copy.653
  493.6 2.0 copy.652
  495.7 3.1 collective-permute-start.43
  500.5 4.3 collective-permute-start.49
  505.9 4.0 collective-permute-start.30
  511.0 2.8 collective-permute-start.32
  514.9 4.8 collective-permute-start.35
  520.9 7.3 %collective-permute-start.39 = (f32[256,256]{1,0:T(8,128)S(1)}, f32[256,256]{1,0:T(8,128)S(1)}, u32[]{:S(2)}, u32[]{:S(2)}) collective-permute-start(f32[256,256]{1,0:T(8,128)S(1)} %slice.2481), channel_id=1, source_target_pairs={{0,32},{4,36},{8,40},{12,44},{16,48},{20,52},{24,56},{28,60},{32,0... | collective-permute-start | bytes 786440 | tf_op jit(solution)/shard_map/ppermute | solution.py:11
  528.3 3.4 collective-permute-start.44
  531.9 3.9 collective-permute-start.50
  536.5 6.9 %collective-permute-done.32 = f32[256,256]{1,0:T(8,128)S(1)} collective-permute-done((f32[256,256]{1,0:T(8,128)S(1)}, f32[256,256]{1,0:T(8,128)S(1)}, u32[]{:S(2)}, u32[]{:S(2)}) %collective-permute-start.32) | collective-permute-done | bytes 262176 | tf_op jit(solution)/shard_map/ppermute | solution.py:11
  545.4 20.2 %collective-permute-done.35 = f32[256,256]{1,0:T(8,128)S(1)} collective-permute-done((f32[256,256]{1,0:T(8,128)S(1)}, f32[256,256]{1,0:T(8,128)S(1)}, u32[]{:S(2)}, u32[]{:S(2)}) %collective-permute-start.35) | collective-permute-done | bytes 262176 | tf_op jit(solution)/shard_map/ppermute | solution.py:11
  569.7 7.9 %collective-permute-start.45 = (f32[128,256]{1,0:T(8,128)S(1)}, f32[128,256]{1,0:T(8,128)S(1)}, u32[]{:S(2)}, u32[]{:S(2)}) collective-permute-start(f32[128,256]{1,0:T(8,128)S(1)} %slice.2495), channel_id=1, source_target_pairs={{0,32},{4,36},{8,40},{12,44},{16,48},{20,52},{24,56},{28,60},{32,0... | collective-permute-start | bytes 393224 | tf_op jit(solution)/shard_map/ppermute | solution.py:11
  577.7 3.2 collective-permute-start.51
  581.9 9.4 %collective-permute-start.37 = (f32[64,256]{1,0:T(8,128)S(1)}, f32[64,256]{1,0:T(8,128)S(1)}, u32[]{:S(2)}, u32[]{:S(2)}) collective-permute-start(f32[64,256]{1,0:T(8,128)S(1)} %slice.2475), channel_id=1, source_target_pairs={{0,4},{4,0},{8,12},{12,8},{16,20},{20,16},{24,28},{28,24},{32,36},... | collective-permute-start | bytes 196616 | tf_op jit(solution)/shard_map/ppermute | solution.py:11
  591.3 3.3 collective-permute-done.40
  596.6 10.3 %collective-permute-start.46 = (f32[64,256]{1,0:T(8,128)S(1)}, f32[64,256]{1,0:T(8,128)S(1)}, u32[]{:S(2)}, u32[]{:S(2)}) collective-permute-start(f32[64,256]{1,0:T(8,128)S(1)} %slice.2497), channel_id=1, source_target_pairs={{0,16},{4,20},{8,24},{12,28},{16,0},{20,4},{24,8},{28,12},{32,48},... | collective-permute-start | bytes 196616 | tf_op jit(solution)/shard_map/ppermute | solution.py:11
  607.0 6.5 %collective-permute-start.52 = (f32[64,256]{1,0:T(8,128)S(1)}, f32[64,256]{1,0:T(8,128)S(1)}, u32[]{:S(2)}, u32[]{:S(2)}) collective-permute-start(f32[64,256]{1,0:T(8,128)S(1)} %slice.2511), channel_id=1, source_target_pairs={{0,32},{4,36},{8,40},{12,44},{16,48},{20,52},{24,56},{28,60},{32,0... | collective-permute-start | bytes 196616 | tf_op jit(solution)/shard_map/ppermute | solution.py:11
  618.2 4.9 collective-permute-done.52
  623.2 2.5 collective-permute-start.53
  628.4 4.5 collective-permute-done.53
  632.9 2.3 collective-permute-start.54
  636.0 3.5 collective-permute-done.54
  641.4 3.6 collective-permute-done.55
  (947 shorter events, 229.7 us)
Async XLA Ops:
  1.9 19.7 %copy-start.72 = (bf16[4,128]{1,0:T(4,128)(2,1)}, bf16[4,128]{1,0:T(4,128)(2,1)S(1)}, u32[]{:S(2)}) copy-start(bf16[4,128]{1,0:T(4,128)(2,1)S(1)} %get-tuple-element.1147) | copy-start | bytes 3076
  2.0 19.7 %copy-start.74 = (bf16[4,128]{1,0:T(4,128)(2,1)}, bf16[4,128]{1,0:T(4,128)(2,1)S(1)}, u32[]{:S(2)}) copy-start(bf16[4,128]{1,0:T(4,128)(2,1)S(1)} %get-tuple-element.1148) | copy-start | bytes 3076
  2.0 19.7 %copy-start.76 = (bf16[4,128]{1,0:T(4,128)(2,1)}, bf16[4,128]{1,0:T(4,128)(2,1)S(1)}, u32[]{:S(2)}) copy-start(bf16[4,128]{1,0:T(4,128)(2,1)S(1)} %get-tuple-element.1149) | copy-start | bytes 3076
  2.0 19.7 %copy-start.78 = (bf16[4,128]{1,0:T(4,128)(2,1)}, bf16[4,128]{1,0:T(4,128)(2,1)S(1)}, u32[]{:S(2)}) copy-start(bf16[4,128]{1,0:T(4,128)(2,1)S(1)} %get-tuple-element.1150) | copy-start | bytes 3076
  2.6 77.4 %collective-permute-start.21 = (bf16[8,256]{1,0:T(8,128)(2,1)}, bf16[8,256]{1,0:T(8,128)(2,1)S(1)}, u32[]{:S(2)}, u32[]{:S(2)}) collective-permute-start(bf16[8,256]{1,0:T(8,128)(2,1)} %maximum_maximum_fusion.4), channel_id=1, source_target_pairs={{0,4},{4,0},{8,12},{12,8},{16,20},{20,16},{24,28},{28,24},{32,36},... | collective-permute-start | bytes 12296 | tf_op jit(solution)/shard_map/ppermute | solution.py:11
  6.5 15.9 %copy-start.59 = (bf16[8,128]{1,0:T(8,128)(2,1)}, bf16[8,128]{1,0:T(8,128)(2,1)S(1)}, u32[]{:S(2)}) copy-start(bf16[8,128]{1,0:T(8,128)(2,1)S(1)} %get-tuple-element.1143) | copy-start | bytes 6148
  7.7 74.3 %collective-permute-start.15 = (bf16[16,256]{1,0:T(8,128)(2,1)}, bf16[16,256]{1,0:T(8,128)(2,1)}, u32[]{:S(2)}, u32[]{:S(2)}) collective-permute-start(bf16[16,256]{1,0:T(8,128)(2,1)} %maximum_maximum_fusion.3), channel_id=1, source_target_pairs={{0,4},{4,0},{8,12},{12,8},{16,20},{20,16},{24,28},{28,24},{32,36},... | collective-permute-start | bytes 24584 | tf_op jit(solution)/shard_map/ppermute | solution.py:11
  10.5 82.7 %collective-permute-start.10 = (bf16[32,256]{1,0:T(8,128)(2,1)}, bf16[32,256]{1,0:T(8,128)(2,1)S(1)}, u32[]{:S(2)}, u32[]{:S(2)}) collective-permute-start(bf16[32,256]{1,0:T(8,128)(2,1)} %maximum_maximum_fusion.2), channel_id=1, source_target_pairs={{0,4},{4,0},{8,12},{12,8},{16,20},{20,16},{24,28},{28,24},{32,36},... | collective-permute-start | bytes 49160 | tf_op jit(solution)/shard_map/ppermute | solution.py:11
  15.0 99.9 %collective-permute-start.6 = (bf16[64,256]{1,0:T(8,128)(2,1)}, bf16[64,256]{1,0:T(8,128)(2,1)S(1)}, u32[]{:S(2)}, u32[]{:S(2)}) collective-permute-start(bf16[64,256]{1,0:T(8,128)(2,1)} %maximum_maximum_fusion.1), channel_id=1, source_target_pairs={{0,4},{4,0},{8,12},{12,8},{16,20},{20,16},{24,28},{28,24},{32,36},... | collective-permute-start | bytes 98312 | tf_op jit(solution)/shard_map/ppermute | solution.py:11
  17.8 124.0 %collective-permute-start.3 = (bf16[128,256]{1,0:T(8,128)(2,1)}, bf16[128,256]{1,0:T(8,128)(2,1)S(1)}, u32[]{:S(2)}, u32[]{:S(2)}) collective-permute-start(bf16[128,256]{1,0:T(8,128)(2,1)} %maximum_maximum_fusion), channel_id=1, source_target_pairs={{0,4},{4,0},{8,12},{12,8},{16,20},{20,16},{24,28},{28,24},{32,36},... | collective-permute-start | bytes 196616 | tf_op jit(solution)/shard_map/ppermute | solution.py:11
  42.4 140.0 %copy-start.95 = (s32[128]{0:T(128)}, s32[128]{0:T(128)S(1)}, u32[]{:S(2)}) copy-start(s32[128]{0:T(128)S(1)} %convert_reduce_fusion.20) | copy-start | bytes 1540
  80.0 103.8 %collective-permute-start.1 = (bf16[256,256]{1,0:T(8,128)(2,1)}, bf16[256,256]{1,0:T(8,128)(2,1)}, u32[]{:S(2)}, u32[]{:S(2)}) collective-permute-start(bf16[256,256]{1,0:T(8,128)(2,1)} %pad_maximum_fusion.26), channel_id=1, source_target_pairs={{0,4},{4,0},{8,12},{12,8},{16,20},{20,16},{24,28},{28,24},{32,36},... | collective-permute-start | bytes 393224 | tf_op jit(solution)/shard_map/ppermute | solution.py:11
  82.1 7.2 %collective-permute-start.22 = (bf16[16,256]{1,0:T(8,128)(2,1)S(1)}, bf16[16,256]{1,0:T(8,128)(2,1)S(1)}, u32[]{:S(2)}, u32[]{:S(2)}) collective-permute-start(bf16[16,256]{1,0:T(8,128)(2,1)S(1)} %pad_maximum_fusion.39), channel_id=1, source_target_pairs={{0,8},{4,12},{8,0},{12,4},{16,24},{20,28},{24,16},{28,20},{32,40},... | collective-permute-start | bytes 24584 | tf_op jit(solution)/shard_map/ppermute | solution.py:11
  89.3 86.7 %collective-permute-start = (bf16[256,256]{1,0:T(8,128)(2,1)S(1)}, bf16[256,256]{1,0:T(8,128)(2,1)S(1)}, u32[]{:S(2)}, u32[]{:S(2)}) collective-permute-start(bf16[256,256]{1,0:T(8,128)(2,1)S(1)} %pad_maximum_fusion.25), channel_id=1, source_target_pairs={{0,4},{4,0},{8,12},{12,8},{16,20},{20,16},{24,28},{28,24},{32,36},... | collective-permute-start | bytes 393224 | tf_op jit(solution)/shard_map/ppermute | solution.py:11
  93.2 6.5 %collective-permute-start.16 = (bf16[32,256]{1,0:T(8,128)(2,1)S(1)}, bf16[32,256]{1,0:T(8,128)(2,1)S(1)}, u32[]{:S(2)}, u32[]{:S(2)}) collective-permute-start(bf16[32,256]{1,0:T(8,128)(2,1)S(1)} %pad_maximum_fusion.35), channel_id=1, source_target_pairs={{0,8},{4,12},{8,0},{12,4},{16,24},{20,28},{24,16},{28,20},{32,40},... | collective-permute-start | bytes 49160 | tf_op jit(solution)/shard_map/ppermute | solution.py:11
  99.7 10.8 %collective-permute-start.23 = (bf16[32,256]{1,0:T(8,128)(2,1)S(1)}, bf16[32,256]{1,0:T(8,128)(2,1)S(1)}, u32[]{:S(2)}, u32[]{:S(2)}) collective-permute-start(bf16[32,256]{1,0:T(8,128)(2,1)S(1)} %pad_maximum_fusion.36), channel_id=1, source_target_pairs={{0,16},{4,20},{8,24},{12,28},{16,0},{20,4},{24,8},{28,12},{32,48},... | collective-permute-start | bytes 49160 | tf_op jit(solution)/shard_map/ppermute | solution.py:11
  110.5 13.0 %collective-permute-start.11 = (bf16[64,256]{1,0:T(8,128)(2,1)S(1)}, bf16[64,256]{1,0:T(8,128)(2,1)S(1)}, u32[]{:S(2)}, u32[]{:S(2)}) collective-permute-start(bf16[64,256]{1,0:T(8,128)(2,1)S(1)} %pad_maximum_fusion.31), channel_id=1, source_target_pairs={{0,8},{4,12},{8,0},{12,4},{16,24},{20,28},{24,16},{28,20},{32,40},... | collective-permute-start | bytes 98312 | tf_op jit(solution)/shard_map/ppermute | solution.py:11
  114.9 17.4 %collective-permute-start.17 = (bf16[64,256]{1,0:T(8,128)(2,1)S(1)}, bf16[64,256]{1,0:T(8,128)(2,1)S(1)}, u32[]{:S(2)}, u32[]{:S(2)}) collective-permute-start(bf16[64,256]{1,0:T(8,128)(2,1)S(1)} %pad_maximum_fusion.32), channel_id=1, source_target_pairs={{0,16},{4,20},{8,24},{12,28},{16,0},{20,4},{24,8},{28,12},{32,48},... | collective-permute-start | bytes 98312 | tf_op jit(solution)/shard_map/ppermute | solution.py:11
  123.5 14.6 %collective-permute-start.24 = (bf16[64,256]{1,0:T(8,128)(2,1)S(1)}, bf16[64,256]{1,0:T(8,128)(2,1)S(1)}, u32[]{:S(2)}, u32[]{:S(2)}) collective-permute-start(bf16[64,256]{1,0:T(8,128)(2,1)S(1)} %concatenate.419), channel_id=1, source_target_pairs={{0,32},{4,36},{8,40},{12,44},{16,48},{20,52},{24,56},{28,60},{32,0... | collective-permute-start | bytes 98312 | tf_op jit(solution)/shard_map/ppermute | solution.py:11
  132.3 20.4 %collective-permute-start.7 = (bf16[128,256]{1,0:T(8,128)(2,1)S(1)}, bf16[128,256]{1,0:T(8,128)(2,1)S(1)}, u32[]{:S(2)}, u32[]{:S(2)}) collective-permute-start(bf16[128,256]{1,0:T(8,128)(2,1)S(1)} %pad_maximum_fusion.29), channel_id=1, source_target_pairs={{0,8},{4,12},{8,0},{12,4},{16,24},{20,28},{24,16},{28,20},{32,40},... | collective-permute-start | bytes 196616 | tf_op jit(solution)/shard_map/ppermute | solution.py:11
  138.1 19.4 %collective-permute-start.12 = (bf16[128,256]{1,0:T(8,128)(2,1)S(1)}, bf16[128,256]{1,0:T(8,128)(2,1)S(1)}, u32[]{:S(2)}, u32[]{:S(2)}) collective-permute-start(bf16[128,256]{1,0:T(8,128)(2,1)S(1)} %pad_maximum_fusion.30), channel_id=1, source_target_pairs={{0,16},{4,20},{8,24},{12,28},{16,0},{20,4},{24,8},{28,12},{32,48},... | collective-permute-start | bytes 196616 | tf_op jit(solution)/shard_map/ppermute | solution.py:11
  141.8 19.4 %collective-permute-start.18 = (bf16[128,256]{1,0:T(8,128)(2,1)}, bf16[128,256]{1,0:T(8,128)(2,1)S(1)}, u32[]{:S(2)}, u32[]{:S(2)}) collective-permute-start(bf16[128,256]{1,0:T(8,128)(2,1)} %get-tuple-element.952), channel_id=1, source_target_pairs={{0,32},{4,36},{8,40},{12,44},{16,48},{20,52},{24,56},{28,60},{32,0... | collective-permute-start | bytes 196616 | tf_op jit(solution)/shard_map/ppermute | solution.py:11
  152.7 13.5 %collective-permute-start.25 = (bf16[128,256]{1,0:T(8,128)(2,1)S(1)}, bf16[128,256]{1,0:T(8,128)(2,1)S(1)}, u32[]{:S(2)}, u32[]{:S(2)}) collective-permute-start(bf16[128,256]{1,0:T(8,128)(2,1)S(1)} %concatenate.420), channel_id=1, source_target_pairs={{0,64},{4,68},{8,72},{12,76},{16,80},{20,84},{24,88},{28,92},{32,9... | collective-permute-start | bytes 196616 | tf_op jit(solution)/shard_map/ppermute | solution.py:11
  157.5 32.7 %collective-permute-start.4 = (bf16[256,256]{1,0:T(8,128)(2,1)}, bf16[256,256]{1,0:T(8,128)(2,1)S(1)}, u32[]{:S(2)}, u32[]{:S(2)}) collective-permute-start(bf16[256,256]{1,0:T(8,128)(2,1)} %pad_maximum_fusion.27), channel_id=1, source_target_pairs={{0,8},{4,12},{8,0},{12,4},{16,24},{20,28},{24,16},{28,20},{32,40},... | collective-permute-start | bytes 393224 | tf_op jit(solution)/shard_map/ppermute | solution.py:11
  161.2 32.7 %collective-permute-start.8 = (bf16[256,256]{1,0:T(8,128)(2,1)}, bf16[256,256]{1,0:T(8,128)(2,1)}, u32[]{:S(2)}, u32[]{:S(2)}) collective-permute-start(bf16[256,256]{1,0:T(8,128)(2,1)} %pad_maximum_fusion.28), channel_id=1, source_target_pairs={{0,16},{4,20},{8,24},{12,28},{16,0},{20,4},{24,8},{28,12},{32,48},... | collective-permute-start | bytes 393224 | tf_op jit(solution)/shard_map/ppermute | solution.py:11
  166.2 35.6 %collective-permute-start.13 = (bf16[256,256]{1,0:T(8,128)(2,1)}, bf16[256,256]{1,0:T(8,128)(2,1)}, u32[]{:S(2)}, u32[]{:S(2)}) collective-permute-start(bf16[256,256]{1,0:T(8,128)(2,1)} %get-tuple-element.938), channel_id=1, source_target_pairs={{0,32},{4,36},{8,40},{12,44},{16,48},{20,52},{24,56},{28,60},{32,0... | collective-permute-start | bytes 393224 | tf_op jit(solution)/shard_map/ppermute | solution.py:11
  176.0 34.7 %collective-permute-start.19 = (bf16[256,256]{1,0:T(8,128)(2,1)}, bf16[256,256]{1,0:T(8,128)(2,1)}, u32[]{:S(2)}, u32[]{:S(2)}) collective-permute-start(bf16[256,256]{1,0:T(8,128)(2,1)} %get-tuple-element.935), channel_id=1, source_target_pairs={{0,64},{4,68},{8,72},{12,76},{16,80},{20,84},{24,88},{28,92},{32,9... | collective-permute-start | bytes 393224 | tf_op jit(solution)/shard_map/ppermute | solution.py:11
  184.4 30.6 %collective-permute-start.26 = (bf16[256,256]{1,0:T(8,128)(2,1)S(1)}, bf16[256,256]{1,0:T(8,128)(2,1)S(1)}, u32[]{:S(2)}, u32[]{:S(2)}) collective-permute-start(bf16[256,256]{1,0:T(8,128)(2,1)S(1)} %copy-done.28), channel_id=1, source_target_pairs={{0,128},{4,132},{8,136},{12,140},{16,144},{20,148},{24,152},{28,15... | collective-permute-start | bytes 393224 | tf_op jit(solution)/shard_map/ppermute | solution.py:11
  190.2 32.8 %collective-permute-start.2 = (bf16[512,256]{1,0:T(8,128)(2,1)S(1)}, bf16[512,256]{1,0:T(8,128)(2,1)}, u32[]{:S(2)}, u32[]{:S(2)}) collective-permute-start(bf16[512,256]{1,0:T(8,128)(2,1)S(1)} %pad_maximum_fusion.20), channel_id=1, source_target_pairs={{0,8},{4,12},{8,0},{12,4},{16,24},{20,28},{24,16},{28,20},{32,40},... | collective-permute-start | bytes 786440 | tf_op jit(solution)/shard_map/ppermute | solution.py:11
  193.8 21.1 %copy-start.5 = (bf16[1024,256]{1,0:T(8,128)(2,1)}, bf16[1024,256]{1,0:T(8,128)(2,1)S(1)}, u32[]{:S(2)}) copy-start(bf16[1024,256]{1,0:T(8,128)(2,1)S(1)} %constant_dynamic-update-slice_fusion.1) | copy-start | bytes 1572868
  193.9 64.8 %collective-permute-start.5 = (bf16[512,256]{1,0:T(8,128)(2,1)}, bf16[512,256]{1,0:T(8,128)(2,1)}, u32[]{:S(2)}, u32[]{:S(2)}) collective-permute-start(bf16[512,256]{1,0:T(8,128)(2,1)} %pad_maximum_fusion.21), channel_id=1, source_target_pairs={{0,16},{4,20},{8,24},{12,28},{16,0},{20,4},{24,8},{28,12},{32,48},... | collective-permute-start | bytes 786440 | tf_op jit(solution)/shard_map/ppermute | solution.py:11
  201.8 21.2 %copy-start.7 = (bf16[1024,256]{1,0:T(8,128)(2,1)}, bf16[1024,256]{1,0:T(8,128)(2,1)S(1)}, u32[]{:S(2)}) copy-start(bf16[1024,256]{1,0:T(8,128)(2,1)S(1)} %get-tuple-element.926) | copy-start | bytes 1572868
  201.8 73.8 %collective-permute-start.9 = (bf16[512,256]{1,0:T(8,128)(2,1)}, bf16[512,256]{1,0:T(8,128)(2,1)}, u32[]{:S(2)}, u32[]{:S(2)}) collective-permute-start(bf16[512,256]{1,0:T(8,128)(2,1)} %get-tuple-element.925), channel_id=1, source_target_pairs={{0,32},{4,36},{8,40},{12,44},{16,48},{20,52},{24,56},{28,60},{32,0... | collective-permute-start | bytes 786440 | tf_op jit(solution)/shard_map/ppermute | solution.py:11
  210.7 86.6 %collective-permute-start.14 = (bf16[512,256]{1,0:T(8,128)(2,1)}, bf16[512,256]{1,0:T(8,128)(2,1)}, u32[]{:S(2)}, u32[]{:S(2)}) collective-permute-start(bf16[512,256]{1,0:T(8,128)(2,1)} %get-tuple-element.923), channel_id=1, source_target_pairs={{0,64},{4,68},{8,72},{12,76},{16,80},{20,84},{24,88},{28,92},{32,9... | collective-permute-start | bytes 786440 | tf_op jit(solution)/shard_map/ppermute | solution.py:11
  215.0 109.6 %collective-permute-start.20 = (bf16[512,256]{1,0:T(8,128)(2,1)}, bf16[512,256]{1,0:T(8,128)(2,1)}, u32[]{:S(2)}, u32[]{:S(2)}) collective-permute-start(bf16[512,256]{1,0:T(8,128)(2,1)} %get-tuple-element.921), channel_id=1, source_target_pairs={{0,128},{4,132},{8,136},{12,140},{16,144},{20,148},{24,152},{28,15... | collective-permute-start | bytes 786440 | tf_op jit(solution)/shard_map/ppermute | solution.py:11
  223.1 129.8 %collective-permute-start.27 = (bf16[512,256]{1,0:T(8,128)(2,1)}, bf16[512,256]{1,0:T(8,128)(2,1)}, u32[]{:S(2)}, u32[]{:S(2)}) collective-permute-start(bf16[512,256]{1,0:T(8,128)(2,1)} %concatenate.422), channel_id=1, source_target_pairs={{0,256},{4,260},{8,264},{12,268},{16,272},{20,276},{24,280},{28,28... | collective-permute-start | bytes 786440 | tf_op jit(solution)/shard_map/ppermute | solution.py:11
  258.6 241.8 %collective-permute-start.29 = (f32[512,256]{0,1:T(8,128)}, f32[512,256]{0,1:T(8,128)}, u32[]{:S(2)}, u32[]{:S(2)}) collective-permute-start(f32[512,256]{0,1:T(8,128)} %slice.2212), channel_id=1, source_target_pairs={{0,8},{4,12},{8,0},{12,4},{16,24},{20,28},{24,16},{28,20},{32,40},... | collective-permute-start | bytes 1572872 | tf_op jit(solution)/shard_map/ppermute | solution.py:11
  275.6 220.1 %collective-permute-start.28 = (f32[256,256]{0,1:T(8,128)}, f32[256,256]{0,1:T(8,128)}, u32[]{:S(2)}, u32[]{:S(2)}) collective-permute-start(f32[256,256]{0,1:T(8,128)} %bitcast.622), channel_id=1, source_target_pairs={{0,4},{4,0},{8,12},{12,8},{16,20},{20,16},{24,28},{28,24},{32,36},... | collective-permute-start | bytes 786440 | tf_op jit(solution)/shard_map/ppermute | solution.py:11
  297.4 208.5 %collective-permute-start.31 = (f32[512,256]{1,0:T(8,128)}, f32[512,256]{1,0:T(8,128)}, u32[]{:S(2)}, u32[]{:S(2)}) collective-permute-start(f32[512,256]{1,0:T(8,128)} %bitcast.190), channel_id=1, source_target_pairs={{0,16},{4,20},{8,24},{12,28},{16,0},{20,4},{24,8},{28,12},{32,48},... | collective-permute-start | bytes 1572872 | tf_op jit(solution)/shard_map/ppermute | solution.py:11
  324.6 186.4 %collective-permute-start.34 = (f32[512,256]{1,0:T(8,128)}, f32[512,256]{1,0:T(8,128)}, u32[]{:S(2)}, u32[]{:S(2)}) collective-permute-start(f32[512,256]{1,0:T(8,128)} %bitcast.694), channel_id=1, source_target_pairs={{0,32},{4,36},{8,40},{12,44},{16,48},{20,52},{24,56},{28,60},{32,0... | collective-permute-start | bytes 1572872 | tf_op jit(solution)/shard_map/ppermute | solution.py:11
  352.8 162.1 %collective-permute-start.38 = (f32[512,256]{1,0:T(8,128)}, f32[512,256]{1,0:T(8,128)}, u32[]{:S(2)}, u32[]{:S(2)}) collective-permute-start(f32[512,256]{1,0:T(8,128)} %bitcast.206), channel_id=1, source_target_pairs={{0,64},{4,68},{8,72},{12,76},{16,80},{20,84},{24,88},{28,92},{32,9... | collective-permute-start | bytes 1572872 | tf_op jit(solution)/shard_map/ppermute | solution.py:11
  495.7 25.2 %collective-permute-start.43 = (f32[512,256]{1,0:T(8,128)}, f32[512,256]{1,0:T(8,128)S(1)}, u32[]{:S(2)}, u32[]{:S(2)}) collective-permute-start(f32[512,256]{1,0:T(8,128)} %bitcast.695), channel_id=1, source_target_pairs={{0,128},{4,132},{8,136},{12,140},{16,144},{20,148},{24,152},{28,15... | collective-permute-start | bytes 1572872 | tf_op jit(solution)/shard_map/ppermute | solution.py:11
  500.5 27.8 %collective-permute-start.49 = (f32[512,256]{1,0:T(8,128)S(1)}, f32[512,256]{1,0:T(8,128)S(1)}, u32[]{:S(2)}, u32[]{:S(2)}) collective-permute-start(f32[512,256]{1,0:T(8,128)S(1)} %copy-done.13), channel_id=1, source_target_pairs={{0,256},{4,260},{8,264},{12,268},{16,272},{20,276},{24,280},{28,28... | collective-permute-start | bytes 1572872 | tf_op jit(solution)/shard_map/ppermute | solution.py:11
  505.9 26.0 %collective-permute-start.30 = (f32[256,256]{0,1:T(8,128)S(1)}, f32[256,256]{0,1:T(8,128)S(1)}, u32[]{:S(2)}, u32[]{:S(2)}) collective-permute-start(f32[256,256]{0,1:T(8,128)S(1)} %slice.2458), channel_id=1, source_target_pairs={{0,4},{4,0},{8,12},{12,8},{16,20},{20,16},{24,28},{28,24},{32,36},... | collective-permute-start | bytes 786440 | tf_op jit(solution)/shard_map/ppermute | solution.py:11
  511.0 32.5 %collective-permute-start.32 = (f32[256,256]{1,0:T(8,128)S(1)}, f32[256,256]{1,0:T(8,128)S(1)}, u32[]{:S(2)}, u32[]{:S(2)}) collective-permute-start(f32[256,256]{1,0:T(8,128)S(1)} %slice.2463), channel_id=1, source_target_pairs={{0,8},{4,12},{8,0},{12,4},{16,24},{20,28},{24,16},{28,20},{32,40},... | collective-permute-start | bytes 786440 | tf_op jit(solution)/shard_map/ppermute | solution.py:11
  514.9 50.7 %collective-permute-start.35 = (f32[256,256]{1,0:T(8,128)S(1)}, f32[256,256]{1,0:T(8,128)S(1)}, u32[]{:S(2)}, u32[]{:S(2)}) collective-permute-start(f32[256,256]{1,0:T(8,128)S(1)} %slice.2471), channel_id=1, source_target_pairs={{0,16},{4,20},{8,24},{12,28},{16,0},{20,4},{24,8},{28,12},{32,48},... | collective-permute-start | bytes 786440 | tf_op jit(solution)/shard_map/ppermute | solution.py:11
  520.9 46.8 %collective-permute-start.39 = (f32[256,256]{1,0:T(8,128)S(1)}, f32[256,256]{1,0:T(8,128)S(1)}, u32[]{:S(2)}, u32[]{:S(2)}) collective-permute-start(f32[256,256]{1,0:T(8,128)S(1)} %slice.2481), channel_id=1, source_target_pairs={{0,32},{4,36},{8,40},{12,44},{16,48},{20,52},{24,56},{28,60},{32,0... | collective-permute-start | bytes 786440 | tf_op jit(solution)/shard_map/ppermute | solution.py:11
  528.3 41.3 %collective-permute-start.44 = (f32[256,256]{1,0:T(8,128)S(1)}, f32[256,256]{1,0:T(8,128)S(1)}, u32[]{:S(2)}, u32[]{:S(2)}) collective-permute-start(f32[256,256]{1,0:T(8,128)S(1)} %slice.2493), channel_id=1, source_target_pairs={{0,64},{4,68},{8,72},{12,76},{16,80},{20,84},{24,88},{28,92},{32,9... | collective-permute-start | bytes 786440 | tf_op jit(solution)/shard_map/ppermute | solution.py:11
  531.9 45.8 %collective-permute-start.50 = (f32[256,256]{1,0:T(8,128)S(1)}, f32[256,256]{1,0:T(8,128)S(1)}, u32[]{:S(2)}, u32[]{:S(2)}) collective-permute-start(f32[256,256]{1,0:T(8,128)S(1)} %slice.2507), channel_id=1, source_target_pairs={{0,128},{4,132},{8,136},{12,140},{16,144},{20,148},{24,152},{28,15... | collective-permute-start | bytes 786440 | tf_op jit(solution)/shard_map/ppermute | solution.py:11
  543.5 37.4 %collective-permute-start.33 = (f32[128,256]{1,0:T(8,128)S(1)}, f32[128,256]{1,0:T(8,128)S(1)}, u32[]{:S(2)}, u32[]{:S(2)}) collective-permute-start(f32[128,256]{1,0:T(8,128)S(1)} %slice.2465), channel_id=1, source_target_pairs={{0,4},{4,0},{8,12},{12,8},{16,20},{20,16},{24,28},{28,24},{32,36},... | collective-permute-start | bytes 393224 | tf_op jit(solution)/shard_map/ppermute | solution.py:11
  565.7 16.2 %collective-permute-start.36 = (f32[128,256]{1,0:T(8,128)S(1)}, f32[128,256]{1,0:T(8,128)S(1)}, u32[]{:S(2)}, u32[]{:S(2)}) collective-permute-start(f32[128,256]{1,0:T(8,128)S(1)} %slice.2473), channel_id=1, source_target_pairs={{0,8},{4,12},{8,0},{12,4},{16,24},{20,28},{24,16},{28,20},{32,40},... | collective-permute-start | bytes 393224 | tf_op jit(solution)/shard_map/ppermute | solution.py:11
  567.7 26.9 %collective-permute-start.40 = (f32[128,256]{1,0:T(8,128)S(1)}, f32[128,256]{1,0:T(8,128)S(1)}, u32[]{:S(2)}, u32[]{:S(2)}) collective-permute-start(f32[128,256]{1,0:T(8,128)S(1)} %slice.2483), channel_id=1, source_target_pairs={{0,16},{4,20},{8,24},{12,28},{16,0},{20,4},{24,8},{28,12},{32,48},... | collective-permute-start | bytes 393224 | tf_op jit(solution)/shard_map/ppermute | solution.py:11
  569.7 26.8 %collective-permute-start.45 = (f32[128,256]{1,0:T(8,128)S(1)}, f32[128,256]{1,0:T(8,128)S(1)}, u32[]{:S(2)}, u32[]{:S(2)}) collective-permute-start(f32[128,256]{1,0:T(8,128)S(1)} %slice.2495), channel_id=1, source_target_pairs={{0,32},{4,36},{8,40},{12,44},{16,48},{20,52},{24,56},{28,60},{32,0... | collective-permute-start | bytes 393224 | tf_op jit(solution)/shard_map/ppermute | solution.py:11
  577.7 29.2 %collective-permute-start.51 = (f32[128,256]{1,0:T(8,128)S(1)}, f32[128,256]{1,0:T(8,128)S(1)}, u32[]{:S(2)}, u32[]{:S(2)}) collective-permute-start(f32[128,256]{1,0:T(8,128)S(1)} %slice.2509), channel_id=1, source_target_pairs={{0,64},{4,68},{8,72},{12,76},{16,80},{20,84},{24,88},{28,92},{32,9... | collective-permute-start | bytes 393224 | tf_op jit(solution)/shard_map/ppermute | solution.py:11
  581.9 31.6 %collective-permute-start.37 = (f32[64,256]{1,0:T(8,128)S(1)}, f32[64,256]{1,0:T(8,128)S(1)}, u32[]{:S(2)}, u32[]{:S(2)}) collective-permute-start(f32[64,256]{1,0:T(8,128)S(1)} %slice.2475), channel_id=1, source_target_pairs={{0,4},{4,0},{8,12},{12,8},{16,20},{20,16},{24,28},{28,24},{32,36},... | collective-permute-start | bytes 196616 | tf_op jit(solution)/shard_map/ppermute | solution.py:11
  594.6 19.7 %collective-permute-start.41 = (f32[64,256]{1,0:T(8,128)S(1)}, f32[64,256]{1,0:T(8,128)S(1)}, u32[]{:S(2)}, u32[]{:S(2)}) collective-permute-start(f32[64,256]{1,0:T(8,128)S(1)} %slice.2485), channel_id=1, source_target_pairs={{0,8},{4,12},{8,0},{12,4},{16,24},{20,28},{24,16},{28,20},{32,40},... | collective-permute-start | bytes 196616 | tf_op jit(solution)/shard_map/ppermute | solution.py:11
  596.6 19.7 %collective-permute-start.46 = (f32[64,256]{1,0:T(8,128)S(1)}, f32[64,256]{1,0:T(8,128)S(1)}, u32[]{:S(2)}, u32[]{:S(2)}) collective-permute-start(f32[64,256]{1,0:T(8,128)S(1)} %slice.2497), channel_id=1, source_target_pairs={{0,16},{4,20},{8,24},{12,28},{16,0},{20,4},{24,8},{28,12},{32,48},... | collective-permute-start | bytes 196616 | tf_op jit(solution)/shard_map/ppermute | solution.py:11
  607.0 16.2 %collective-permute-start.52 = (f32[64,256]{1,0:T(8,128)S(1)}, f32[64,256]{1,0:T(8,128)S(1)}, u32[]{:S(2)}, u32[]{:S(2)}) collective-permute-start(f32[64,256]{1,0:T(8,128)S(1)} %slice.2511), channel_id=1, source_target_pairs={{0,32},{4,36},{8,40},{12,44},{16,48},{20,52},{24,56},{28,60},{32,0... | collective-permute-start | bytes 196616 | tf_op jit(solution)/shard_map/ppermute | solution.py:11
  614.4 11.4 %collective-permute-start.42 = (f32[32,256]{1,0:T(8,128)S(1)}, f32[32,256]{1,0:T(8,128)S(1)}, u32[]{:S(2)}, u32[]{:S(2)}) collective-permute-start(f32[32,256]{1,0:T(8,128)S(1)} %slice.2487), channel_id=1, source_target_pairs={{0,4},{4,0},{8,12},{12,8},{16,20},{20,16},{24,28},{28,24},{32,36},... | collective-permute-start | bytes 98312 | tf_op jit(solution)/shard_map/ppermute | solution.py:11
  616.3 10.2 %collective-permute-start.47 = (f32[32,256]{1,0:T(8,128)S(1)}, f32[32,256]{1,0:T(8,128)S(1)}, u32[]{:S(2)}, u32[]{:S(2)}) collective-permute-start(f32[32,256]{1,0:T(8,128)S(1)} %slice.2499), channel_id=1, source_target_pairs={{0,8},{4,12},{8,0},{12,4},{16,24},{20,28},{24,16},{28,20},{32,40},... | collective-permute-start | bytes 98312 | tf_op jit(solution)/shard_map/ppermute | solution.py:11
  623.2 9.7 %collective-permute-start.53 = (f32[32,256]{1,0:T(8,128)S(1)}, f32[32,256]{1,0:T(8,128)S(1)}, u32[]{:S(2)}, u32[]{:S(2)}) collective-permute-start(f32[32,256]{1,0:T(8,128)S(1)} %slice.2513), channel_id=1, source_target_pairs={{0,16},{4,20},{8,24},{12,28},{16,0},{20,4},{24,8},{28,12},{32,48},... | collective-permute-start | bytes 98312 | tf_op jit(solution)/shard_map/ppermute | solution.py:11
  626.5 8.8 %collective-permute-start.48 = (f32[16,256]{1,0:T(8,128)S(1)}, f32[16,256]{1,0:T(8,128)S(1)}, u32[]{:S(2)}, u32[]{:S(2)}) collective-permute-start(f32[16,256]{1,0:T(8,128)S(1)} %slice.2501), channel_id=1, source_target_pairs={{0,4},{4,0},{8,12},{12,8},{16,20},{20,16},{24,28},{28,24},{32,36},... | collective-permute-start | bytes 49160 | tf_op jit(solution)/shard_map/ppermute | solution.py:11
  632.9 6.5 %collective-permute-start.54 = (f32[16,256]{1,0:T(8,128)S(1)}, f32[16,256]{1,0:T(8,128)S(1)}, u32[]{:S(2)}, u32[]{:S(2)}) collective-permute-start(f32[16,256]{1,0:T(8,128)S(1)} %slice.2515), channel_id=1, source_target_pairs={{0,8},{4,12},{8,0},{12,4},{16,24},{20,28},{24,16},{28,20},{32,40},... | collective-permute-start | bytes 49160 | tf_op jit(solution)/shard_map/ppermute | solution.py:11
  639.5 5.5 collective-permute-start.55
  (157 other events, 262.2 us)
